TPU v7x, 512 devices: a whole 4x8x8 slice. The times are simulated.
512 devices in a mesh: grp: 8 (over y), sub: 64 (over x, z, core).
Axes of the slice: x: 4, y: 8, z: 8, core: 2. Of those that a mesh axis runs over, the one named last changes fastest.
Arguments:
- omega: bfloat16 [393216, 256], P(('grp', 'sub')), may hold values from -6 to 6
- adj_tests: bfloat16 [256, 393216], P('sub', 'grp'), may hold values from -6 to 6
- near_tiles: bfloat16 [3072, 12, 128, 128], P(('grp', 'sub')), may hold values from -0.15625 to 0.15625
- tile_cols: int32 [3072, 12], P(('grp', 'sub')), may hold values from 0 to 3071, as said below
- leaf_perms: int32 [512, 2, 768], P(('grp', 'sub')), may hold values from 0 to 767, each once within a row
- leaf_interp: bfloat16 [512, 2, 672, 96], P(('grp', 'sub')), may hold values from -0.125 to 0.125
- node_perms: int32 [512, 9, 2, 192], P(('grp', 'sub')), may hold values from 0 to 191, as said below
- node_maps: bfloat16 [512, 9, 4, 96, 96], P(('grp', 'sub')), as said below
Outputs:
- path_panels: bfloat16 [512, 9, 2, 96, 256], P(('grp', 'sub'))
Inputs may be any that keep to these rules, and one draw needn't show every extreme that they name: `tile_cols`: the 12 column tiles of tile row q are distinct and lie in the tile rows of its own leaf or of the leaves just before and after it within the same block of 64 leaves; each block of 64 leaves is one index of grp. `leaf_perms`: each of the two orders of a leaf is a permutation of 0 to 767. `node_perms`: each order is a permutation of 0 to 191; entries [d, j] are equal for all d with the same d // 2^(j+1). `node_maps`: entries [d, j] are equal for all d with the same d // 2^(j+1).
All inputs are finite; a program needn't handle non-finite values.
Results may differ from a plain program's by a relative error of at most 0.0065.
Values may be sent and summed in bfloat16 or wider, within the bound.
A program may use at most 64 MiB of HBM per device.

v0:
```python
import jax
import jax.numpy as jnp
from jax import lax
from jax.sharding import PartitionSpec as P

HIGHEST = lax.Precision.HIGHEST


def extended(block, sides, width):
    for axis, dim in sides:
        count = lax.axis_size(axis)
        forward = [(i, i + 1) for i in range(count - 1)]
        backward = [(target, source) for source, target in forward]
        low = lax.ppermute(
            lax.slice_in_dim(block, block.shape[dim] - width, None, axis=dim), axis, forward
        )
        high = lax.ppermute(lax.slice_in_dim(block, 0, width, axis=dim), axis, backward)
        block = jnp.concatenate([low, block, high], axis=dim)
    return block


def passed_along(block, axis, distance):
    devices = range(lax.axis_size(axis))
    route = [(i - distance, i) for i in devices if i - distance in devices]
    return lax.ppermute(block, axis, route)


def partner_2(block, axis, distance):
    count = lax.axis_size(axis)
    route = []
    for low in range(count):
        high = low | 1 << distance
        if high != low and high < count:
            route += [(low, high), (high, low)]
    return lax.ppermute(block, axis, route)


def for_sending(x):
    return jax.tree.map(lambda a: a.astype(jnp.bfloat16) if a.dtype == jnp.float32 else a, x)


def apply_rows(matrix, panel):
    return jnp.einsum("...ij,...js->...is", matrix, panel, precision=HIGHEST)


def apply_cols(matrix, panel):
    return jnp.einsum("...ji,...js->...is", matrix, panel, precision=HIGHEST)


def pick_rows(panel, order):
    return jnp.take_along_axis(panel, order[..., None], axis=-2)


def squeeze_node(
    fwd_rows, fwd_tests, adj_rows, adj_panel, row_order, col_order, row_interp, col_interp
):
    rank = row_interp.shape[-1]
    fwd_skel = pick_rows(fwd_rows, row_order[..., :rank])
    test_skel = pick_rows(fwd_tests, col_order[..., :rank]) + apply_cols(
        col_interp, pick_rows(fwd_tests, col_order[..., rank:])
    )
    adj_skel = pick_rows(adj_rows, col_order[..., :rank])
    adj_test_skel = pick_rows(adj_panel, row_order[..., :rank]) + apply_cols(
        row_interp, pick_rows(adj_panel, row_order[..., rank:])
    )
    return (fwd_skel, test_skel, adj_skel, adj_test_skel)


def merge_pair(lower, upper, maps, orders):
    maps = maps.astype(jnp.float32)
    row_interp = maps[..., 0, :, :]
    col_interp = maps[..., 1, :, :]
    low_high = maps[..., 2, :, :]
    high_low = maps[..., 3, :, :]
    fwd_rows = jnp.concatenate(
        [lower[0] - apply_rows(low_high, upper[1]), upper[0] - apply_rows(high_low, lower[1])],
        axis=-2,
    )
    fwd_tests = jnp.concatenate([lower[1], upper[1]], axis=-2)
    adj_rows = jnp.concatenate(
        [lower[2] - apply_cols(high_low, upper[3]), upper[2] - apply_cols(low_high, lower[3])],
        axis=-2,
    )
    adj_panel = jnp.concatenate([lower[3], upper[3]], axis=-2)
    return squeeze_node(
        fwd_rows,
        fwd_tests,
        adj_rows,
        adj_panel,
        orders[..., 0, :],
        orders[..., 1, :],
        row_interp,
        col_interp,
    )


def pair_up(panels, partner, upper_side):
    lower = tuple((jnp.where(upper_side, b, a) for a, b in zip(panels, partner)))
    upper = tuple((jnp.where(upper_side, a, b) for a, b in zip(panels, partner)))
    return (lower, upper)


def local(omega, adj_tests, near_tiles, tile_cols, leaf_perms, leaf_interp, node_perms, node_maps):
    rows_dev, samples = omega.shape
    tile_size = near_tiles.shape[-1]
    per_dev = rows_dev // tile_size
    sub_count = lax.axis_size("sub")
    sub_place = lax.axis_index("sub")
    grp_place = lax.axis_index("grp")
    device = grp_place * sub_count + sub_place
    local_cols = tile_cols - (device - 1) * per_dev
    widened = extended(omega, (("sub", 0),), rows_dev)
    blocks = widened.reshape(3 * per_dev, tile_size, samples)
    picked = jnp.take(blocks, local_cols, axis=0)
    forward = jnp.einsum(
        "rtij,rtjs->ris", near_tiles, picked, preferred_element_type=jnp.float32
    ).reshape(rows_dev, samples)
    adj_cols = lax.all_to_all(adj_tests, "sub", split_axis=1, concat_axis=0, tiled=True)
    adj_blocks = adj_cols.reshape(samples, per_dev, tile_size)
    onehot = (
        local_cols[:, :, None] == jnp.arange(3 * per_dev, dtype=jnp.int32)[None, None, :]
    ).astype(jnp.bfloat16)
    placed = jnp.einsum(
        "rtk,rtij->rkij", onehot, near_tiles, preferred_element_type=jnp.float32
    ).astype(jnp.bfloat16)
    spread = jnp.einsum("rkij,sri->kjs", placed, adj_blocks, preferred_element_type=jnp.float32)
    lower_rim = spread[:per_dev].reshape(rows_dev, samples)
    own_part = spread[per_dev : 2 * per_dev].reshape(rows_dev, samples)
    upper_rim = spread[2 * per_dev :].reshape(rows_dev, samples)
    from_after = passed_along(lower_rim.astype(jnp.bfloat16), "sub", -1).astype(lower_rim.dtype)
    from_before = passed_along(upper_rim.astype(jnp.bfloat16), "sub", 1).astype(upper_rim.dtype)
    adjoint = own_part + from_after + from_before
    rank = leaf_interp.shape[-1]
    row_order = leaf_perms[0, 0]
    col_order = leaf_perms[0, 1]
    fwd_skel = forward[row_order[:rank]]
    test_skel = omega[col_order[:rank]].astype(jnp.float32) + lax.dot_general(
        leaf_interp[0, 1],
        omega[col_order[rank:]],
        (((0,), (0,)), ((), ())),
        preferred_element_type=jnp.float32,
    )
    adj_skel = adjoint[col_order[:rank]]
    ordered = jnp.take(adj_cols, row_order, axis=1)
    adj_test_skel = ordered[:, :rank].T.astype(jnp.float32) + lax.dot_general(
        leaf_interp[0, 0],
        ordered[:, rank:],
        (((0,), (1,)), ((), ())),
        preferred_element_type=jnp.float32,
    )
    panels = (fwd_skel, test_skel, adj_skel, adj_test_skel)
    sub_bits = lax.axis_size("sub").bit_length() - 1
    grp_bits = lax.axis_size("grp").bit_length() - 1
    results = []
    for bit in range(sub_bits):
        partner = partner_2((panels[0], panels[1], panels[2], panels[3]), "sub", bit)
        upper_side = jnp.right_shift(sub_place, bit) & 1 == 1
        lower, upper = pair_up(panels, partner, upper_side)
        panels = merge_pair(lower, upper, node_maps[0, bit], node_perms[0, bit])
        results.append(jnp.stack([panels[0], panels[2]]).astype(jnp.bfloat16))
    for bit in range(grp_bits):
        partner = partner_2(
            (
                for_sending(panels[0]),
                for_sending(panels[1]),
                for_sending(panels[2]),
                for_sending(panels[3]),
            ),
            "grp",
            bit,
        )
        upper_side = jnp.right_shift(grp_place, bit) & 1 == 1
        lower, upper = pair_up(panels, partner, upper_side)
        level = sub_bits + bit
        panels = merge_pair(lower, upper, node_maps[0, level], node_perms[0, level])
        results.append(jnp.stack([panels[0], panels[2]]).astype(jnp.bfloat16))
    return jnp.stack(results)[None]


def solution(mesh):
    placed = (
        P(("grp", "sub"), None),
        P("sub", "grp"),
        P(("grp", "sub"), None, None, None),
        P(("grp", "sub"), None),
        P(("grp", "sub"), None, None),
        P(("grp", "sub"), None, None, None),
        P(("grp", "sub"), None, None, None),
        P(("grp", "sub"), None, None, None, None),
    )
    return jax.shard_map(
        local,
        mesh=mesh,
        in_specs=placed,
        out_specs=P(("grp", "sub"), None, None, None, None),
        check_vma=False,
    )
```

profile of v0, /device:TPU:56, one launch (start us, length us, event | category | flops | bytes accessed | tf_op | source)
XLA Modules:
  0.0 430.0 jit_solution(3925851073607392825)
XLA Ops:
  1.6 3.8 collective-permute-start
  5.3 16.0 %all-to-all-start = ((bf16[4,64,768]{2,0,1:T(4,128)(2,1)}), bf16[4,64,768]{2,0,1:T(4,128)(2,1)S(1)}, u32[]{:S(2)}, u32[]{:S(2)}) async-start(bf16[4,64,768]{2,0,1:T(4,128)(2,1)} %bitcast.926), calls=%async_computation | async-start | bytes 786432 | tf_op jit(solution)/shard_map/all_to_all | solution.py:118
  24.2 3.3 gather_fusion.3
  34.7 3.8 fusion.5
  38.5 6.7 %copy.16 = bf16[6,18,128,128]{2,3,0,1:T(8,128)(2,1)} copy(bf16[6,18,128,128]{3,1,2,0:T(8,128)(2,1)} %fusion.5) | data formatting | bytes 7077888 | tf_op jit(solution)/shard_map/rtk,rtij->rkij/dot_general | solution.py:123
  63.4 3.5 collective-permute-start.9
  68.2 2.3 collective-permute-done.9
  73.9 4.4 %collective-permute-start.13 = (f32[96,256]{1,0:T(8,128)S(1)}, f32[96,256]{1,0:T(8,128)S(1)}, u32[]{:S(2)}, u32[]{:S(2)}) collective-permute-start(f32[96,256]{1,0:T(8,128)S(1)} %select_add_fusion.9), channel_id=1, source_target_pairs={{0,4},{4,0},{1,5},{5,1},{2,6},{6,2},{3,7},{7,3},{8,12},{12,8},{9,1... | collective-permute-start | bytes 294920 | tf_op jit(solution)/shard_map/ppermute | solution.py:35
  79.4 3.6 collective-permute-done.13
  87.2 7.3 %collective-permute-start.17 = (f32[96,256]{1,0:T(8,128)S(1)}, f32[96,256]{1,0:T(8,128)S(1)}, u32[]{:S(2)}, u32[]{:S(2)}) collective-permute-start(f32[96,256]{1,0:T(8,128)S(1)} %select_add_fusion.7), channel_id=1, source_target_pairs={{0,8},{8,0},{1,9},{9,1},{2,10},{10,2},{3,11},{11,3},{4,12},{12,4},... | collective-permute-start | bytes 294920 | tf_op jit(solution)/shard_map/ppermute | solution.py:35
  95.9 3.9 collective-permute-done.17
  105.3 3.4 collective-permute-start.21
  108.7 2.2 pad_maximum_fusion
  110.9 6.9 %gather_fusion = bf16[72,128,256]{2,1,0:T(8,128)(2,1)} fusion(bf16[18,128,256]{2,1,0:T(8,128)(2,1)} %bitcast.921, s32[1024]{0:T(1024)} %pad_clamp_fusion.38), kind=kCustom, calls=%fused_computation.50 | custom fusion | bytes 9437472 | tf_op jit(solution)/shard_map/jit(_take)/gather | solution.py:114
  117.8 4.3 %fusion = f32[6,256,128,1]{1,2,3,0:T(8,128)} fusion(bf16[6,12,128,128]{3,2,1,0:T(8,128)(2,1)S(1)} %copy-done, bf16[6,12,128,256]{3,2,1,0:T(8,128)(2,1)} %bitcast.922, pred[6,12]{1,0:T(8,128)(4,1)S(1)} %copy-done.51), kind=kOutput, calls=%fused_computation.56 | convolution fusion | flops 606339072 | bytes 7864392 | tf_op jit(solution)/shard_map/rtij,rtjs->ris/dot_general | solution.py:115
  132.5 4.8 %collective-permute-start.25 = (f32[96,256]{1,0:T(8,128)}, f32[96,256]{1,0:T(8,128)}, u32[]{:S(2)}, u32[]{:S(2)}) collective-permute-start(f32[96,256]{1,0:T(8,128)} %select_add_fusion.3), channel_id=1, source_target_pairs={{0,32},{32,0},{1,33},{33,1},{2,34},{34,2},{3,35},{35,3},{4,36},{36... | collective-permute-start | bytes 294920 | tf_op jit(solution)/shard_map/ppermute | solution.py:35
  149.5 3.2 collective-permute-start.29
  157.2 4.7 %collective-permute-start.12 = (f32[96,256]{1,0:T(8,128)S(1)}, f32[96,256]{1,0:T(8,128)}, u32[]{:S(2)}, u32[]{:S(2)}) collective-permute-start(f32[96,256]{1,0:T(8,128)S(1)} %get-tuple-element.19), channel_id=1, source_target_pairs={{0,4},{4,0},{1,5},{5,1},{2,6},{6,2},{3,7},{7,3},{8,12},{12,8},{9,1... | collective-permute-start | bytes 294920 | tf_op jit(solution)/shard_map/ppermute | solution.py:35
  167.0 4.2 collective-permute-start.33
  175.5 4.4 %collective-permute-start.16 = (f32[96,256]{1,0:T(8,128)}, f32[96,256]{1,0:T(8,128)}, u32[]{:S(2)}, u32[]{:S(2)}) collective-permute-start(f32[96,256]{1,0:T(8,128)} %get-tuple-element.15), channel_id=1, source_target_pairs={{0,8},{8,0},{1,9},{9,1},{2,10},{10,2},{3,11},{11,3},{4,12},{12,4},... | collective-permute-start | bytes 294920 | tf_op jit(solution)/shard_map/ppermute | solution.py:35
  188.0 3.3 fusion.342
  196.8 3.4 gather_fusion.5
  203.1 3.1 collective-permute-start.7
  211.8 5.2 %collective-permute-start.20 = (f32[96,256]{1,0:T(8,128)}, f32[96,256]{1,0:T(8,128)}, u32[]{:S(2)}, u32[]{:S(2)}) collective-permute-start(f32[96,256]{1,0:T(8,128)} %get-tuple-element.11), channel_id=1, source_target_pairs={{0,16},{16,0},{1,17},{17,1},{2,18},{18,2},{3,19},{19,3},{4,20},{20... | collective-permute-start | bytes 294920 | tf_op jit(solution)/shard_map/ppermute | solution.py:35
  231.0 3.5 collective-permute-start.24
  241.0 3.2 collective-permute-start.15
  248.1 3.5 collective-permute-start.28
  259.5 4.5 %collective-permute-start.32 = (bf16[96,256]{1,0:T(8,128)(2,1)}, bf16[96,256]{1,0:T(8,128)(2,1)}, u32[]{:S(2)}, u32[]{:S(2)}) collective-permute-start(bf16[96,256]{1,0:T(8,128)(2,1)} %select_convert_fusion.5), channel_id=1, source_target_pairs={{0,128},{128,0},{64,192},{192,64},{256,384},{384,256},{320,448},{4... | collective-permute-start | bytes 147464 | tf_op jit(solution)/shard_map/ppermute | solution.py:35
  270.4 3.9 collective-permute-start.19
  277.5 5.9 %collective-permute-start.36 = (bf16[96,256]{1,0:T(8,128)(2,1)S(1)}, bf16[96,256]{1,0:T(8,128)(2,1)S(1)}, u32[]{:S(2)}, u32[]{:S(2)}) collective-permute-start(bf16[96,256]{1,0:T(8,128)(2,1)S(1)} %select_convert_fusion.3), channel_id=1, source_target_pairs={{0,256},{256,0},{64,320},{320,64},{128,384},{384,128},{192,448},{4... | collective-permute-start | bytes 147464 | tf_op jit(solution)/shard_map/ppermute | solution.py:35
  284.2 3.6 collective-permute-done.36
  292.1 2.2 fusion.17
  301.9 2.7 collective-permute-start.23
  308.3 2.6 collective-permute-start.10
  316.6 6.3 %collective-permute-start.27 = (f32[96,256]{1,0:T(8,128)}, f32[96,256]{1,0:T(8,128)S(1)}, u32[]{:S(2)}, u32[]{:S(2)}) collective-permute-start(f32[96,256]{1,0:T(8,128)} %select_add_fusion.2), channel_id=1, source_target_pairs={{0,32},{32,0},{1,33},{33,1},{2,34},{34,2},{3,35},{35,3},{4,36},{36... | collective-permute-start | bytes 294920 | tf_op jit(solution)/shard_map/ppermute | solution.py:35
  327.3 4.8 %collective-permute-start.14 = (f32[96,256]{1,0:T(8,128)}, f32[96,256]{1,0:T(8,128)}, u32[]{:S(2)}, u32[]{:S(2)}) collective-permute-start(f32[96,256]{1,0:T(8,128)} %get-tuple-element.21), channel_id=1, source_target_pairs={{0,4},{4,0},{1,5},{5,1},{2,6},{6,2},{3,7},{7,3},{8,12},{12,8},{9,1... | collective-permute-start | bytes 294920 | tf_op jit(solution)/shard_map/ppermute | solution.py:35
  335.8 3.5 collective-permute-start.31
  353.2 3.5 collective-permute-start.18
  363.8 8.3 %collective-permute-start.39 = (bf16[96,256]{1,0:T(8,128)(2,1)}, bf16[96,256]{1,0:T(8,128)(2,1)}, u32[]{:S(2)}, u32[]{:S(2)}) collective-permute-start(bf16[96,256]{1,0:T(8,128)(2,1)} %get-tuple-element.142), channel_id=1, source_target_pairs={{0,256},{256,0},{64,320},{320,64},{128,384},{384,128},{192,448},{4... | collective-permute-start | bytes 147464 | tf_op jit(solution)/shard_map/ppermute | solution.py:35
  376.1 2.7 collective-permute-start.22
  380.3 2.3 collective-permute-done.22
  385.5 3.6 collective-permute-start.26
  390.6 3.0 collective-permute-done.26
  396.8 2.1 collective-permute-start.30
  399.5 3.2 collective-permute-done.30
  405.8 2.3 collective-permute-start.34
  408.7 4.1 collective-permute-done.34
  418.4 7.8 %collective-permute-done.38 = bf16[96,256]{1,0:T(8,128)(2,1)S(1)} collective-permute-done((bf16[96,256]{1,0:T(8,128)(2,1)S(1)}, bf16[96,256]{1,0:T(8,128)(2,1)S(1)}, u32[]{:S(2)}, u32[]{:S(2)}) %collective-permute-start.38) | collective-permute-done | bytes 49184 | tf_op jit(solution)/shard_map/ppermute | solution.py:35
  (385 shorter events, 223.5 us)
Async XLA Ops:
  0.0 34.7 %copy-start = (bf16[6,12,128,128]{3,2,1,0:T(8,128)(2,1)S(1)}, bf16[6,12,128,128]{3,2,1,0:T(8,128)(2,1)}, u32[]{:S(2)}) copy-start(bf16[6,12,128,128]{3,2,1,0:T(8,128)(2,1)} %param.12) | copy-start | bytes 7077892
  0.0 24.2 %copy-start.1 = (bf16[768,256]{1,0:T(8,128)(2,1)S(1)}, bf16[768,256]{1,0:T(8,128)(2,1)}, u32[]{:S(2)}) copy-start(bf16[768,256]{1,0:T(8,128)(2,1)} %param.10) | copy-start | bytes 1179652
  0.0 108.7 %collective-permute-start.1 = (bf16[768,256]{1,0:T(8,128)(2,1)}, bf16[768,256]{1,0:T(8,128)(2,1)}, u32[]{:S(2)}, u32[]{:S(2)}) collective-permute-start(bf16[768,256]{1,0:T(8,128)(2,1)} %param.10), channel_id=1, source_target_pairs={{1,0},{2,1},{3,2},{4,3},{5,4},{6,5},{7,6},{8,7},{9,8},{10,9},{11,1... | collective-permute-start | bytes 1179656 | tf_op jit(solution)/shard_map/ppermute | solution.py:17
  1.6 107.2 %collective-permute-start = (bf16[768,256]{1,0:T(8,128)(2,1)}, bf16[768,256]{1,0:T(8,128)(2,1)}, u32[]{:S(2)}, u32[]{:S(2)}) collective-permute-start(bf16[768,256]{1,0:T(8,128)(2,1)} %param.10), channel_id=1, source_target_pairs={{0,1},{1,2},{2,3},{3,4},{4,5},{5,6},{6,7},{7,8},{8,9},{9,10},{10,1... | collective-permute-start | bytes 1179656 | tf_op jit(solution)/shard_map/ppermute | solution.py:14
  5.3 26.2 %copy-start.45 = (s32[1,2,768]{2,1,0:T(2,128)S(1)}, s32[1,2,768]{2,1,0:T(2,128)}, u32[]{:S(2)}) copy-start(s32[1,2,768]{2,1,0:T(2,128)} %param.14) | copy-start | bytes 18436
  5.3 26.2 %copy-start.44 = (s32[1,9,2,192]{3,2,1,0:T(2,128)S(1)}, s32[1,9,2,192]{3,2,1,0:T(2,128)}, u32[]{:S(2)}) copy-start(s32[1,9,2,192]{3,2,1,0:T(2,128)} %param.16) | copy-start | bytes 41476
  5.3 180.8 %all-to-all-start = ((bf16[4,64,768]{2,0,1:T(4,128)(2,1)}), bf16[4,64,768]{2,0,1:T(4,128)(2,1)S(1)}, u32[]{:S(2)}, u32[]{:S(2)}) async-start(bf16[4,64,768]{2,0,1:T(4,128)(2,1)} %bitcast.926), calls=%async_computation | async-start | bytes 786432 | tf_op jit(solution)/shard_map/all_to_all | solution.py:118
  29.5 30.6 %collective-permute-start.3 = (f32[96,256]{1,0:T(8,128)S(1)}, f32[96,256]{1,0:T(8,128)S(1)}, u32[]{:S(2)}, u32[]{:S(2)}) collective-permute-start(f32[96,256]{1,0:T(8,128)S(1)} %fusion.16), channel_id=1, source_target_pairs={{0,1},{1,0},{2,3},{3,2},{4,5},{5,4},{6,7},{7,6},{8,9},{9,8},{10,11... | collective-permute-start | bytes 294920 | tf_op jit(solution)/shard_map/ppermute | solution.py:35
  63.4 7.0 %collective-permute-start.9 = (f32[96,256]{1,0:T(8,128)S(1)}, f32[96,256]{1,0:T(8,128)S(1)}, u32[]{:S(2)}, u32[]{:S(2)}) collective-permute-start(f32[96,256]{1,0:T(8,128)S(1)} %select_add_fusion.11), channel_id=1, source_target_pairs={{0,2},{2,0},{1,3},{3,1},{4,6},{6,4},{5,7},{7,5},{8,10},{10,8},{9,1... | collective-permute-start | bytes 294920 | tf_op jit(solution)/shard_map/ppermute | solution.py:35
  73.9 9.2 %collective-permute-start.13 = (f32[96,256]{1,0:T(8,128)S(1)}, f32[96,256]{1,0:T(8,128)S(1)}, u32[]{:S(2)}, u32[]{:S(2)}) collective-permute-start(f32[96,256]{1,0:T(8,128)S(1)} %select_add_fusion.9), channel_id=1, source_target_pairs={{0,4},{4,0},{1,5},{5,1},{2,6},{6,2},{3,7},{7,3},{8,12},{12,8},{9,1... | collective-permute-start | bytes 294920 | tf_op jit(solution)/shard_map/ppermute | solution.py:35
  87.2 12.5 %collective-permute-start.17 = (f32[96,256]{1,0:T(8,128)S(1)}, f32[96,256]{1,0:T(8,128)S(1)}, u32[]{:S(2)}, u32[]{:S(2)}) collective-permute-start(f32[96,256]{1,0:T(8,128)S(1)} %select_add_fusion.7), channel_id=1, source_target_pairs={{0,8},{8,0},{1,9},{9,1},{2,10},{10,2},{3,11},{11,3},{4,12},{12,4},... | collective-permute-start | bytes 294920 | tf_op jit(solution)/shard_map/ppermute | solution.py:35
  105.3 20.8 %collective-permute-start.21 = (f32[96,256]{1,0:T(8,128)}, f32[96,256]{1,0:T(8,128)}, u32[]{:S(2)}, u32[]{:S(2)}) collective-permute-start(f32[96,256]{1,0:T(8,128)} %select_add_fusion.5), channel_id=1, source_target_pairs={{0,16},{16,0},{1,17},{17,1},{2,18},{18,2},{3,19},{19,3},{4,20},{20... | collective-permute-start | bytes 294920 | tf_op jit(solution)/shard_map/ppermute | solution.py:35
  124.1 13.2 %collective-permute-start.2 = (f32[96,256]{1,0:T(8,128)S(1)}, f32[96,256]{1,0:T(8,128)}, u32[]{:S(2)}, u32[]{:S(2)}) collective-permute-start(f32[96,256]{1,0:T(8,128)S(1)} %gather_fusion.1), channel_id=1, source_target_pairs={{0,1},{1,0},{2,3},{3,2},{4,5},{5,4},{6,7},{7,6},{8,9},{9,8},{10,11... | collective-permute-start | bytes 294920 | tf_op jit(solution)/shard_map/ppermute | solution.py:35
  132.5 11.2 %collective-permute-start.25 = (f32[96,256]{1,0:T(8,128)}, f32[96,256]{1,0:T(8,128)}, u32[]{:S(2)}, u32[]{:S(2)}) collective-permute-start(f32[96,256]{1,0:T(8,128)} %select_add_fusion.3), channel_id=1, source_target_pairs={{0,32},{32,0},{1,33},{33,1},{2,34},{34,2},{3,35},{35,3},{4,36},{36... | collective-permute-start | bytes 294920 | tf_op jit(solution)/shard_map/ppermute | solution.py:35
  141.7 11.0 %collective-permute-start.8 = (f32[96,256]{1,0:T(8,128)}, f32[96,256]{1,0:T(8,128)}, u32[]{:S(2)}, u32[]{:S(2)}) collective-permute-start(f32[96,256]{1,0:T(8,128)} %get-tuple-element.23), channel_id=1, source_target_pairs={{0,2},{2,0},{1,3},{3,1},{4,6},{6,4},{5,7},{7,5},{8,10},{10,8},{9,1... | collective-permute-start | bytes 294920 | tf_op jit(solution)/shard_map/ppermute | solution.py:35
  149.5 12.5 %collective-permute-start.29 = (bf16[96,256]{1,0:T(8,128)(2,1)}, bf16[96,256]{1,0:T(8,128)(2,1)}, u32[]{:S(2)}, u32[]{:S(2)}) collective-permute-start(bf16[96,256]{1,0:T(8,128)(2,1)} %get-tuple-element.136), channel_id=1, source_target_pairs={{0,64},{64,0},{128,192},{192,128},{256,320},{320,256},{384,448},{4... | collective-permute-start | bytes 147464 | tf_op jit(solution)/shard_map/ppermute | solution.py:35
  157.2 14.0 %collective-permute-start.12 = (f32[96,256]{1,0:T(8,128)S(1)}, f32[96,256]{1,0:T(8,128)}, u32[]{:S(2)}, u32[]{:S(2)}) collective-permute-start(f32[96,256]{1,0:T(8,128)S(1)} %get-tuple-element.19), channel_id=1, source_target_pairs={{0,4},{4,0},{1,5},{5,1},{2,6},{6,2},{3,7},{7,3},{8,12},{12,8},{9,1... | collective-permute-start | bytes 294920 | tf_op jit(solution)/shard_map/ppermute | solution.py:35
  167.0 12.9 %collective-permute-start.33 = (bf16[96,256]{1,0:T(8,128)(2,1)}, bf16[96,256]{1,0:T(8,128)(2,1)}, u32[]{:S(2)}, u32[]{:S(2)}) collective-permute-start(bf16[96,256]{1,0:T(8,128)(2,1)} %get-tuple-element.140), channel_id=1, source_target_pairs={{0,128},{128,0},{64,192},{192,64},{256,384},{384,256},{320,448},{4... | collective-permute-start | bytes 147464 | tf_op jit(solution)/shard_map/ppermute | solution.py:35
  175.5 30.6 %collective-permute-start.16 = (f32[96,256]{1,0:T(8,128)}, f32[96,256]{1,0:T(8,128)}, u32[]{:S(2)}, u32[]{:S(2)}) collective-permute-start(f32[96,256]{1,0:T(8,128)} %get-tuple-element.15), channel_id=1, source_target_pairs={{0,8},{8,0},{1,9},{9,1},{2,10},{10,2},{3,11},{11,3},{4,12},{12,4},... | collective-permute-start | bytes 294920 | tf_op jit(solution)/shard_map/ppermute | solution.py:35
  184.2 100.0 %collective-permute-start.37 = (bf16[96,256]{1,0:T(8,128)(2,1)}, bf16[96,256]{1,0:T(8,128)(2,1)}, u32[]{:S(2)}, u32[]{:S(2)}) collective-permute-start(bf16[96,256]{1,0:T(8,128)(2,1)} %get-tuple-element.144), channel_id=1, source_target_pairs={{0,256},{256,0},{64,320},{320,64},{128,384},{384,128},{192,448},{4... | collective-permute-start | bytes 147464 | tf_op jit(solution)/shard_map/ppermute | solution.py:35
  192.3 99.8 %collective-permute-start.5 = (bf16[768,256]{1,0:T(8,128)(2,1)}, bf16[768,256]{1,0:T(8,128)(2,1)}, u32[]{:S(2)}, u32[]{:S(2)}) collective-permute-start(bf16[768,256]{1,0:T(8,128)(2,1)} %bitcast.32), channel_id=1, source_target_pairs={{0,1},{1,2},{2,3},{3,4},{4,5},{5,6},{6,7},{7,8},{8,9},{9,10},{10,1... | collective-permute-start | bytes 1179656 | tf_op jit(solution)/shard_map/ppermute | solution.py:25
  194.3 97.8 %collective-permute-start.4 = (bf16[768,256]{1,0:T(8,128)(2,1)}, bf16[768,256]{1,0:T(8,128)(2,1)}, u32[]{:S(2)}, u32[]{:S(2)}) collective-permute-start(bf16[768,256]{1,0:T(8,128)(2,1)} %bitcast.31), channel_id=1, source_target_pairs={{1,0},{2,1},{3,2},{4,3},{5,4},{6,5},{7,6},{8,7},{9,8},{10,9},{11,1... | collective-permute-start | bytes 1179656 | tf_op jit(solution)/shard_map/ppermute | solution.py:25
  203.1 14.0 %collective-permute-start.7 = (f32[96,256]{1,0:T(8,128)}, f32[96,256]{1,0:T(8,128)}, u32[]{:S(2)}, u32[]{:S(2)}) collective-permute-start(f32[96,256]{1,0:T(8,128)} %fusion.15), channel_id=1, source_target_pairs={{0,1},{1,0},{2,3},{3,2},{4,5},{5,4},{6,7},{7,6},{8,9},{9,8},{10,11... | collective-permute-start | bytes 294920 | tf_op jit(solution)/shard_map/ppermute | solution.py:35
  211.8 13.6 %collective-permute-start.20 = (f32[96,256]{1,0:T(8,128)}, f32[96,256]{1,0:T(8,128)}, u32[]{:S(2)}, u32[]{:S(2)}) collective-permute-start(f32[96,256]{1,0:T(8,128)} %get-tuple-element.11), channel_id=1, source_target_pairs={{0,16},{16,0},{1,17},{17,1},{2,18},{18,2},{3,19},{19,3},{4,20},{20... | collective-permute-start | bytes 294920 | tf_op jit(solution)/shard_map/ppermute | solution.py:35
  223.5 11.0 %collective-permute-start.11 = (f32[96,256]{1,0:T(8,128)}, f32[96,256]{1,0:T(8,128)}, u32[]{:S(2)}, u32[]{:S(2)}) collective-permute-start(f32[96,256]{1,0:T(8,128)} %select_add_fusion.10), channel_id=1, source_target_pairs={{0,2},{2,0},{1,3},{3,1},{4,6},{6,4},{5,7},{7,5},{8,10},{10,8},{9,1... | collective-permute-start | bytes 294920 | tf_op jit(solution)/shard_map/ppermute | solution.py:35
  231.0 13.2 %collective-permute-start.24 = (f32[96,256]{1,0:T(8,128)}, f32[96,256]{1,0:T(8,128)}, u32[]{:S(2)}, u32[]{:S(2)}) collective-permute-start(f32[96,256]{1,0:T(8,128)} %get-tuple-element.7), channel_id=1, source_target_pairs={{0,32},{32,0},{1,33},{33,1},{2,34},{34,2},{3,35},{35,3},{4,36},{36... | collective-permute-start | bytes 294920 | tf_op jit(solution)/shard_map/ppermute | solution.py:35
  241.0 23.0 %collective-permute-start.15 = (f32[96,256]{1,0:T(8,128)}, f32[96,256]{1,0:T(8,128)}, u32[]{:S(2)}, u32[]{:S(2)}) collective-permute-start(f32[96,256]{1,0:T(8,128)} %select_add_fusion.8), channel_id=1, source_target_pairs={{0,4},{4,0},{1,5},{5,1},{2,6},{6,2},{3,7},{7,3},{8,12},{12,8},{9,1... | collective-permute-start | bytes 294920 | tf_op jit(solution)/shard_map/ppermute | solution.py:35
  248.1 6.0 %collective-permute-start.28 = (bf16[96,256]{1,0:T(8,128)(2,1)S(1)}, bf16[96,256]{1,0:T(8,128)(2,1)S(1)}, u32[]{:S(2)}, u32[]{:S(2)}) collective-permute-start(bf16[96,256]{1,0:T(8,128)(2,1)S(1)} %select_convert_fusion.7), channel_id=1, source_target_pairs={{0,64},{64,0},{128,192},{192,128},{256,320},{320,256},{384,448},{4... | collective-permute-start | bytes 147464 | tf_op jit(solution)/shard_map/ppermute | solution.py:35
  259.5 14.9 %collective-permute-start.32 = (bf16[96,256]{1,0:T(8,128)(2,1)}, bf16[96,256]{1,0:T(8,128)(2,1)}, u32[]{:S(2)}, u32[]{:S(2)}) collective-permute-start(bf16[96,256]{1,0:T(8,128)(2,1)} %select_convert_fusion.5), channel_id=1, source_target_pairs={{0,128},{128,0},{64,192},{192,64},{256,384},{384,256},{320,448},{4... | collective-permute-start | bytes 147464 | tf_op jit(solution)/shard_map/ppermute | solution.py:35
  270.4 27.8 %collective-permute-start.19 = (f32[96,256]{1,0:T(8,128)}, f32[96,256]{1,0:T(8,128)}, u32[]{:S(2)}, u32[]{:S(2)}) collective-permute-start(f32[96,256]{1,0:T(8,128)} %select_add_fusion.6), channel_id=1, source_target_pairs={{0,8},{8,0},{1,9},{9,1},{2,10},{10,2},{3,11},{11,3},{4,12},{12,4},... | collective-permute-start | bytes 294920 | tf_op jit(solution)/shard_map/ppermute | solution.py:35
  277.5 10.2 %collective-permute-start.36 = (bf16[96,256]{1,0:T(8,128)(2,1)S(1)}, bf16[96,256]{1,0:T(8,128)(2,1)S(1)}, u32[]{:S(2)}, u32[]{:S(2)}) collective-permute-start(bf16[96,256]{1,0:T(8,128)(2,1)S(1)} %select_convert_fusion.3), channel_id=1, source_target_pairs={{0,256},{256,0},{64,320},{320,64},{128,384},{384,128},{192,448},{4... | collective-permute-start | bytes 147464 | tf_op jit(solution)/shard_map/ppermute | solution.py:35
  296.3 8.3 %collective-permute-start.6 = (f32[96,256]{1,0:T(8,128)S(1)}, f32[96,256]{1,0:T(8,128)S(1)}, u32[]{:S(2)}, u32[]{:S(2)}) collective-permute-start(f32[96,256]{1,0:T(8,128)S(1)} %gather_fusion.4), channel_id=1, source_target_pairs={{0,1},{1,0},{2,3},{3,2},{4,5},{5,4},{6,7},{7,6},{8,9},{9,8},{10,11... | collective-permute-start | bytes 294920 | tf_op jit(solution)/shard_map/ppermute | solution.py:35
  301.9 10.5 %collective-permute-start.23 = (f32[96,256]{1,0:T(8,128)S(1)}, f32[96,256]{1,0:T(8,128)}, u32[]{:S(2)}, u32[]{:S(2)}) collective-permute-start(f32[96,256]{1,0:T(8,128)S(1)} %select_add_fusion.4), channel_id=1, source_target_pairs={{0,16},{16,0},{1,17},{17,1},{2,18},{18,2},{3,19},{19,3},{4,20},{20... | collective-permute-start | bytes 294920 | tf_op jit(solution)/shard_map/ppermute | solution.py:35
  308.3 14.5 %collective-permute-start.10 = (f32[96,256]{1,0:T(8,128)S(1)}, f32[96,256]{1,0:T(8,128)}, u32[]{:S(2)}, u32[]{:S(2)}) collective-permute-start(f32[96,256]{1,0:T(8,128)S(1)} %get-tuple-element.27), channel_id=1, source_target_pairs={{0,2},{2,0},{1,3},{3,1},{4,6},{6,4},{5,7},{7,5},{8,10},{10,8},{9,1... | collective-permute-start | bytes 294920 | tf_op jit(solution)/shard_map/ppermute | solution.py:35
  316.6 15.5 %collective-permute-start.27 = (f32[96,256]{1,0:T(8,128)}, f32[96,256]{1,0:T(8,128)S(1)}, u32[]{:S(2)}, u32[]{:S(2)}) collective-permute-start(f32[96,256]{1,0:T(8,128)} %select_add_fusion.2), channel_id=1, source_target_pairs={{0,32},{32,0},{1,33},{33,1},{2,34},{34,2},{3,35},{35,3},{4,36},{36... | collective-permute-start | bytes 294920 | tf_op jit(solution)/shard_map/ppermute | solution.py:35
  327.3 21.3 %collective-permute-start.14 = (f32[96,256]{1,0:T(8,128)}, f32[96,256]{1,0:T(8,128)}, u32[]{:S(2)}, u32[]{:S(2)}) collective-permute-start(f32[96,256]{1,0:T(8,128)} %get-tuple-element.21), channel_id=1, source_target_pairs={{0,4},{4,0},{1,5},{5,1},{2,6},{6,2},{3,7},{7,3},{8,12},{12,8},{9,1... | collective-permute-start | bytes 294920 | tf_op jit(solution)/shard_map/ppermute | solution.py:35
  335.8 6.0 %collective-permute-start.31 = (bf16[96,256]{1,0:T(8,128)(2,1)S(1)}, bf16[96,256]{1,0:T(8,128)(2,1)S(1)}, u32[]{:S(2)}, u32[]{:S(2)}) collective-permute-start(bf16[96,256]{1,0:T(8,128)(2,1)S(1)} %get-tuple-element.134), channel_id=1, source_target_pairs={{0,64},{64,0},{128,192},{192,128},{256,320},{320,256},{384,448},{4... | collective-permute-start | bytes 147464 | tf_op jit(solution)/shard_map/ppermute | solution.py:35
  346.7 11.4 %collective-permute-start.35 = (bf16[96,256]{1,0:T(8,128)(2,1)}, bf16[96,256]{1,0:T(8,128)(2,1)}, u32[]{:S(2)}, u32[]{:S(2)}) collective-permute-start(bf16[96,256]{1,0:T(8,128)(2,1)} %get-tuple-element.138), channel_id=1, source_target_pairs={{0,128},{128,0},{64,192},{192,64},{256,384},{384,256},{320,448},{4... | collective-permute-start | bytes 147464 | tf_op jit(solution)/shard_map/ppermute | solution.py:35
  353.2 19.0 %collective-permute-start.18 = (f32[96,256]{1,0:T(8,128)}, f32[96,256]{1,0:T(8,128)}, u32[]{:S(2)}, u32[]{:S(2)}) collective-permute-start(f32[96,256]{1,0:T(8,128)} %get-tuple-element.17), channel_id=1, source_target_pairs={{0,8},{8,0},{1,9},{9,1},{2,10},{10,2},{3,11},{11,3},{4,12},{12,4},... | collective-permute-start | bytes 294920 | tf_op jit(solution)/shard_map/ppermute | solution.py:35
  363.8 21.7 %copy-start.48 = (pred[96]{0:T(512)(128)(4,1)S(1)}, pred[96]{0:T(512)(128)(4,1)}, u32[]{:S(2)}) copy-start(pred[96]{0:T(512)(128)(4,1)} %get-tuple-element.78) | copy-start | bytes 292
  363.8 54.6 %collective-permute-start.39 = (bf16[96,256]{1,0:T(8,128)(2,1)}, bf16[96,256]{1,0:T(8,128)(2,1)}, u32[]{:S(2)}, u32[]{:S(2)}) collective-permute-start(bf16[96,256]{1,0:T(8,128)(2,1)} %get-tuple-element.142), channel_id=1, source_target_pairs={{0,256},{256,0},{64,320},{320,64},{128,384},{384,128},{192,448},{4... | collective-permute-start | bytes 147464 | tf_op jit(solution)/shard_map/ppermute | solution.py:35
  376.1 6.5 %collective-permute-start.22 = (f32[96,256]{1,0:T(8,128)S(1)}, f32[96,256]{1,0:T(8,128)S(1)}, u32[]{:S(2)}, u32[]{:S(2)}) collective-permute-start(f32[96,256]{1,0:T(8,128)S(1)} %get-tuple-element.13), channel_id=1, source_target_pairs={{0,16},{16,0},{1,17},{17,1},{2,18},{18,2},{3,19},{19,3},{4,20},{20... | collective-permute-start | bytes 294920 | tf_op jit(solution)/shard_map/ppermute | solution.py:35
  385.5 8.0 %collective-permute-start.26 = (f32[96,256]{1,0:T(8,128)S(1)}, f32[96,256]{1,0:T(8,128)S(1)}, u32[]{:S(2)}, u32[]{:S(2)}) collective-permute-start(f32[96,256]{1,0:T(8,128)S(1)} %get-tuple-element.9), channel_id=1, source_target_pairs={{0,32},{32,0},{1,33},{33,1},{2,34},{34,2},{3,35},{35,3},{4,36},{36... | collective-permute-start | bytes 294920 | tf_op jit(solution)/shard_map/ppermute | solution.py:35
  396.8 6.0 %collective-permute-start.30 = (bf16[96,256]{1,0:T(8,128)(2,1)S(1)}, bf16[96,256]{1,0:T(8,128)(2,1)S(1)}, u32[]{:S(2)}, u32[]{:S(2)}) collective-permute-start(bf16[96,256]{1,0:T(8,128)(2,1)S(1)} %select_convert_fusion.6), channel_id=1, source_target_pairs={{0,64},{64,0},{128,192},{192,128},{256,320},{320,256},{384,448},{4... | collective-permute-start | bytes 147464 | tf_op jit(solution)/shard_map/ppermute | solution.py:35
  405.6 23.6 %copy-start.50 = (pred[96]{0:T(512)(128)(4,1)S(1)}, pred[96]{0:T(512)(128)(4,1)}, u32[]{:S(2)}) copy-start(pred[96]{0:T(512)(128)(4,1)} %get-tuple-element.63) | copy-start | bytes 292
  405.6 23.7 %copy-start.40 = (bf16[1,1,96,256]{3,2,1,0:T(8,128)(2,1)S(1)}, bf16[1,1,96,256]{3,2,1,0:T(8,128)(2,1)}, u32[]{:S(2)}) copy-start(bf16[1,1,96,256]{3,2,1,0:T(8,128)(2,1)} %fusion.53) | copy-start | bytes 147460
  405.8 7.0 %collective-permute-start.34 = (bf16[96,256]{1,0:T(8,128)(2,1)S(1)}, bf16[96,256]{1,0:T(8,128)(2,1)S(1)}, u32[]{:S(2)}, u32[]{:S(2)}) collective-permute-start(bf16[96,256]{1,0:T(8,128)(2,1)S(1)} %select_convert_fusion.4), channel_id=1, source_target_pairs={{0,128},{128,0},{64,192},{192,64},{256,384},{384,256},{320,448},{4... | collective-permute-start | bytes 147464 | tf_op jit(solution)/shard_map/ppermute | solution.py:35
  415.8 10.4 %collective-permute-start.38 = (bf16[96,256]{1,0:T(8,128)(2,1)S(1)}, bf16[96,256]{1,0:T(8,128)(2,1)S(1)}, u32[]{:S(2)}, u32[]{:S(2)}) collective-permute-start(bf16[96,256]{1,0:T(8,128)(2,1)S(1)} %select_convert_fusion.2), channel_id=1, source_target_pairs={{0,256},{256,0},{64,320},{320,64},{128,384},{384,128},{192,448},{4... | collective-permute-start | bytes 147464 | tf_op jit(solution)/shard_map/ppermute | solution.py:35
  (45 other events, 465.0 us)
where the time goes:
time: 436 us; the launch traced here: 430 us
  starting transfers between devices  155 us (36%)
  local copies, waits for them, and re-layouts  89.1 us (20%)
  matrix products  78.3 us (18%)
  other arithmetic  69.5 us (16%)
  waiting for transfers between devices  36 us (8%)
    ppermute x36, starting transfers between devices, partner_2(): return lax.ppermute(block, axis, route)  131 us
    gather x50, local copies, waits for them, and re-layouts, pick_rows(): return jnp.take_along_axis(panel, order[..., None], axis=-2)  55.4 us
    dot_general x34, matrix products, apply_cols(): return jnp.einsum('...ji,...js->...is', matrix, panel, precision=HIGHEST)  44.3 us
    ppermute x36, waiting for transfers between devices, partner_2(): return lax.ppermute(block, axis, route)  36 us
    dot_general x18, matrix products, apply_rows(): return jnp.einsum('...ij,...js->...is', matrix, panel, precision=HIGHEST)  19.6 us
    gather x26, other arithmetic  16.8 us
    another operation x18, other arithmetic, local(): results.append(jnp.stack([panels[0], panels[2]]).astype(jnp.bfloat16))  16.6 us
    all_to_all x1, starting transfers between devices, local(): lax.all_to_all(adj_tests, 'sub', split_axis=1, concat_axis=0, tiled=True)  16 us
  transfers between devices with their start and end apart: 41, of which 11 were waited for; matrix products, arithmetic and copies ran while one was open for 53% of the time, Pallas kernels for 0%

commit v1 on v0

v1 whole, which is shorter than its diff:
```python
import jax
import jax.numpy as jnp
from jax import lax
from jax.experimental import pallas as pl
from jax.experimental.pallas import tpu as pltpu
from jax.sharding import PartitionSpec as P

BF = jnp.bfloat16
F32 = jnp.float32
MESH = pl.DeviceIdType.MESH
K = 96
LEVELS = 9


def mm(a, b):
    return lax.dot_general(a, b, (((1,), (0,)), ((), ())), preferred_element_type=F32)


def mm_nt(a, b):
    return lax.dot_general(a, b, (((1,), (1,)), ((), ())), preferred_element_type=F32)


def mm_tn(a, b):
    return lax.dot_general(a, b, (((0,), (0,)), ((), ())), preferred_element_type=F32)


def onehot(column, width):
    lanes = lax.broadcasted_iota(jnp.int32, (column.shape[0], width), 1)
    return jnp.where(lanes == column, 1.0, 0.0)


def build_kernel(inv, heads, tails, node_cols, near, interp, maps, wf, wa, gl, op_s, op_h, op_g, placed):
    def place(q, carry):
        for m in range(18):
            t = inv[q, m]
            tile = near[q * 12 + jnp.maximum(t - 1, 0)]
            keep = jnp.where(t > 0, 1.0, 0.0)
            placed[pl.ds(pl.multiple_of(q * 128, 128), 128), m * 128 : (m + 1) * 128] = tile * keep.astype(BF)
        return carry

    lax.fori_loop(0, 6, place, 0)
    wf[...] = mm(onehot(heads[:, 0:1], 768).astype(BF), placed[...]).astype(BF)
    for k, col in enumerate((2, 1, 3)):
        pick = onehot(heads[:, col : col + 1], 768).astype(BF)
        wa[k] = mm_nt(pick, placed[:, k * 768 : (k + 1) * 768]).astype(BF)
    for i in range(2):
        tail = onehot(tails[:, i : i + 1], 768).astype(BF)
        gl[i] = (onehot(heads[:, i : i + 1], 768) + mm_tn(interp[i], tail)).astype(BF)

    def level(j, carry):
        picks = [onehot(node_cols[j][:, i : i + 1], 256) for i in range(2)]
        low_high, high_low = maps[j * 4 + 2], maps[j * 4 + 3]
        for ch in range(2):
            sel = picks[ch][:K].astype(BF)
            tests = picks[1 - ch]
            full = (tests[:K] + mm_tn(maps[j * 4 + 1 - ch], tests[K:].astype(BF))).astype(BF)
            couple = (high_low, low_high) if ch == 0 else (low_high, high_low)
            times = mm if ch == 0 else mm_nt
            for half in range(2):
                at = (j * 2 + ch) * 2 + half
                op_s[at] = sel[:, half * 128 : half * 128 + 128]
                op_g[at] = full[:, half * 128 : half * 128 + 128]
                other = sel[:, (1 - half) * 128 : (1 - half) * 128 + K]
                op_h[at, :, 0:K] = times(other, couple[half]).astype(BF)
        return carry

    lax.fori_loop(0, LEVELS, level, 0)


def vmem():
    return pl.BlockSpec(memory_space=pltpu.VMEM)


def build(inv, heads, tails, node_cols, near, interp, maps):
    ops = jax.ShapeDtypeStruct((LEVELS * 4, K, 128), BF)
    return pl.pallas_call(
        build_kernel,
        out_shape=(
            jax.ShapeDtypeStruct((K, 2304), BF),
            jax.ShapeDtypeStruct((3, K, 768), BF),
            jax.ShapeDtypeStruct((2, K, 768), BF),
            ops,
            ops,
            ops,
        ),
        in_specs=[pl.BlockSpec(memory_space=pltpu.SMEM)] + [vmem()] * 6,
        out_specs=tuple(vmem() for _ in range(6)),
        scratch_shapes=[pltpu.VMEM((768, 2304), BF)],
        compiler_params=pltpu.CompilerParams(vmem_limit_bytes=48 << 20),
        cost_estimate=pl.CostEstimate(flops=2_000_000_000, bytes_accessed=8_000_000, transcendentals=0),
        name="build",
    )(inv, heads, tails, node_cols, near, interp, maps)


def mirror(z):
    return lax.rem(jnp.where(lax.rem(z, 2) == 0, 14 - z, 16 - z), 8)


def tree_kernel(
    om_low, om, om_high, adj, wf, wa, gl, op_s, op_h, op_g,
    out, pan, halo_s, halo_r, s0, r0, hi, lo, rec,
    halo_ss, halo_rs, ss0, rs0, ss, rs, os_s, os_r,
):
    g = lax.axis_index("grp")
    s = lax.axis_index("sub")
    core = lax.rem(s, 2)
    z = lax.rem(s // 2, 8)
    x = s // 16
    z0 = lax.rem(z, 2)
    left, right = lax.rem(s + 63, 64), lax.rem(s + 1, 64)

    def sub_at(xx, zz, cc):
        return (xx * 8 + zz) * 2 + cc

    def flip(v, bit):
        return jnp.where(lax.rem(v // bit, 2) == 0, v + bit, v - bit)

    mate = sub_at(x, z, 1 - core)
    zmate = sub_at(x, flip(z, 1), core)
    cross = sub_at(x, flip(z, 1), 1 - core)
    partners = [
        {"sub": mate},
        {"sub": zmate},
        {"sub": sub_at(x, flip(z, 2), core)},
        {"sub": sub_at(x, mirror(z), core)},
        {"sub": sub_at(flip(x, 1), z, core)},
        {"sub": sub_at(3 - x, z, core)},
        {"grp": flip(g, 1)},
        {"grp": flip(g, 2)},
        {"grp": mirror(g)},
    ]
    bits = [core] + [lax.rem(z // b, 2) for b in (1, 2, 4)] + [lax.rem(x // b, 2) for b in (1, 2)]
    bits += [lax.rem(g // b, 2) for b in (1, 2, 4)]

    barrier = pltpu.get_barrier_semaphore()
    greet = partners + [{"sub": left}, {"sub": right}, {"sub": cross}]
    for who in greet:
        pl.semaphore_signal(barrier, inc=1, device_id=who, device_id_type=MESH)
    pl.semaphore_wait(barrier, len(greet))

    started = []

    def send(src, dst, ssem, rsem, who):
        copy = pltpu.make_async_remote_copy(
            src_ref=src, dst_ref=dst, send_sem=ssem, recv_sem=rsem, device_id=who, device_id_type=MESH
        )
        copy.start()
        started.append(copy)
        return copy

    def cols(which):
        return pl.ds(pl.multiple_of(which * 128, 128), 128)

    halos = []
    for i, k, who in ((0, 0, left), (1, 2, right)):
        halo_s[i] = mm_nt(wa[k], adj[...]).astype(BF)
        halos.append(send(halo_s.at[i], halo_r.at[i], halo_ss.at[i], halo_rs.at[i], {"sub": who}))
    firsts = [None] * 4

    def first(q):
        s0[q] = pan[q, :, cols(1 - core)].astype(BF)
        firsts[q] = send(s0.at[q], r0.at[q], ss0.at[q], rs0.at[q], {"sub": mate})

    pan[1] = mm(gl[1], om[...])
    first(1)
    pan[3] = mm_nt(gl[0], adj[...])
    first(3)
    pan[0] = mm(wf[:, 0:768], om_low[...]) + mm(wf[:, 768:1536], om[...]) + mm(wf[:, 1536:2304], om_high[...])
    first(0)
    own_adj = mm_nt(wa[1], adj[...])
    for copy in halos:
        copy.wait_recv()
    pan[2] = own_adj + halo_r[0].astype(F32) + halo_r[1].astype(F32)
    first(2)

    def split(value):
        top = value.astype(BF)
        return top, (value - top.astype(F32)).astype(BF)

    def twice(op, top, low):
        return mm(op, top) + mm(op, low)

    for ch in range(2):
        f_top, f_low = split(pan[2 * ch, :, cols(core)])
        o_top, o_low = split(pan[2 * ch + 1, :, cols(core)])
        own, far = ch * 2 + core, ch * 2 + 1 - core
        firsts[2 * ch + 1].wait_recv()
        o_far = r0[2 * ch + 1]
        o_new = twice(op_g[own][:, :K], o_top, o_low) + mm(op_g[far][:, :K], o_far)
        hi[0, 2 * ch + 1], lo[2 * ch + 1] = split(o_new)
        f_new = twice(op_s[own][:, :K], f_top, f_low) - twice(op_h[own][:, :K], o_top, o_low)
        f_new = f_new - mm(op_h[far][:, :K], o_far)
        firsts[2 * ch].wait_recv()
        f_new = f_new + mm(op_s[far][:, :K], r0[2 * ch])
        hi[0, 2 * ch], lo[2 * ch] = split(f_new)

    ways = []
    arrivals = []
    for i in (1, 0):
        ways.append(send(hi.at[0, 2 * (1 - z0) + i], rec.at[0, i], ss.at[0, i], rs.at[0, i], partners[1]))
    ways = [ways[1], ways[0]]
    for ch in range(2):
        out[0, ch, :, cols(core)] = hi[0, 2 * ch]
        arrivals.append(
            send(hi.at[0, 2 * ch], out.at[0, ch, :, cols(core)], os_s.at[0, ch], os_r.at[0, ch], partners[0])
        )
    f_top, o_top = hi[0, 2 * z0], hi[0, 2 * z0 + 1]
    f_low, o_low = lo[2 * z0], lo[2 * z0 + 1]
    peers = ({"sub": mate}, {"sub": zmate}, {"sub": cross})
    for j in range(1, LEVELS):
        base = (j * 2 + z0) * 2
        own, far = base + bits[j], base + 1 - bits[j]
        last = j == LEVELS - 1
        o_part = None if last else twice(op_g[own][:, :K], o_top, o_low)
        f_part = twice(op_s[own][:, :K], f_top, f_low) - twice(op_h[own][:, :K], o_top, o_low)
        ways[1].wait_recv()
        o_far = rec[j - 1, 1]
        nexts = [None, None]
        if not last:
            o_top, o_low = split(o_part + mm(op_g[far][:, :K], o_far))
            hi[j, 1] = o_top
            nexts[1] = send(hi.at[j, 1], rec.at[j, 1], ss.at[j, 1], rs.at[j, 1], partners[j + 1])
        f_part = f_part - mm(op_h[far][:, :K], o_far)
        ways[0].wait_recv()
        f_top, f_low = split(f_part + mm(op_s[far][:, :K], rec[j - 1, 0]))
        hi[j, 0] = f_top
        if not last:
            nexts[0] = send(hi.at[j, 0], rec.at[j, 0], ss.at[j, 0], rs.at[j, 0], partners[j + 1])
        for k, who in enumerate(peers):
            arrivals.append(
                send(hi.at[j, 0], out.at[j, z0, :, cols(core)], os_s.at[j, k], os_r.at[j, k], who)
            )
        out[j, z0, :, cols(core)] = f_top
        ways = nexts
    for copy in arrivals:
        copy.wait_recv()
    for copy in started:
        copy.wait_send()


def tree(*args):
    dma = pltpu.SemaphoreType.DMA
    return pl.pallas_call(
        tree_kernel,
        out_shape=jax.ShapeDtypeStruct((LEVELS, 2, K, 256), BF),
        in_specs=[vmem()] * len(args),
        out_specs=vmem(),
        scratch_shapes=[
            pltpu.VMEM((4, K, 256), F32),
            pltpu.VMEM((2, K, 256), BF),
            pltpu.VMEM((2, K, 256), BF),
            pltpu.VMEM((4, K, 128), BF),
            pltpu.VMEM((4, K, 128), BF),
            pltpu.VMEM((LEVELS, 4, K, 128), BF),
            pltpu.VMEM((4, K, 128), BF),
            pltpu.VMEM((LEVELS - 1, 2, K, 128), BF),
            dma((2,)),
            dma((2,)),
            dma((4,)),
            dma((4,)),
            dma((LEVELS, 2)),
            dma((LEVELS, 2)),
            dma((LEVELS, 3)),
            dma((LEVELS, 3)),
        ],
        compiler_params=pltpu.CompilerParams(
            collective_id=0, has_side_effects=True, vmem_limit_bytes=48 << 20
        ),
        name="tree",
    )(*args)


def local(omega, adj_tests, near_tiles, tile_cols, leaf_perms, leaf_interp, node_perms, node_maps):
    device = lax.axis_index("grp") * 64 + lax.axis_index("sub")
    up = [(i, (i + 1) % 64) for i in range(64)]
    down = [(b, a) for a, b in up]
    own_head = leaf_perms[0, 1, :K]
    cols_low = lax.ppermute(own_head, "sub", up)
    cols_high = lax.ppermute(own_head, "sub", down)
    om_low = lax.ppermute(omega, "sub", up)
    om_high = lax.ppermute(omega, "sub", down)
    adj = lax.all_to_all(adj_tests, "sub", split_axis=1, concat_axis=0, tiled=True)
    local_cols = tile_cols - (device - 1) * 6
    slots = jnp.arange(18, dtype=jnp.int32)
    counts = jnp.arange(1, 13, dtype=jnp.int32)
    inv = jnp.sum(
        jnp.where(local_cols[:, :, None] == slots[None, None, :], counts[None, :, None], 0), axis=1
    ).astype(jnp.int32)
    heads = jnp.stack([leaf_perms[0, 0, :K], own_head, cols_low, cols_high], axis=1)
    tails = leaf_perms[0, :, K:].T
    shifted = node_perms[0] + jnp.where(node_perms[0] >= K, 128 - K, 0)
    node_cols = shifted.transpose(0, 2, 1)
    ops = build(
        inv,
        heads,
        tails,
        node_cols,
        near_tiles.reshape(72, 128, 128),
        leaf_interp[0],
        node_maps.reshape(LEVELS * 4, K, K),
    )
    return tree(om_low, omega, om_high, adj, *ops)[None]


def solution(mesh):
    placed = (
        P(("grp", "sub"), None),
        P("sub", "grp"),
        P(("grp", "sub"), None, None, None),
        P(("grp", "sub"), None),
        P(("grp", "sub"), None, None),
        P(("grp", "sub"), None, None, None),
        P(("grp", "sub"), None, None, None),
        P(("grp", "sub"), None, None, None, None),
    )
    return jax.shard_map(
        local,
        mesh=mesh,
        in_specs=placed,
        out_specs=P(("grp", "sub"), None, None, None, None),
        check_vma=False,
    )
```

time: 436 us -> 98.6 us (0.23)
  the two profiles are of different devices: /device:TPU:56 before, /device:TPU:1 now
where the time goes in v1:
time: 98.6 us; the launch traced here: 97.9 us
  Pallas kernels  54.3 us (55%)
  starting transfers between devices  29.7 us (30%)
  local copies, waits for them, and re-layouts  12.8 us (13%)
    pallas_call x1, Pallas kernels, tree(): pl.pallas_call(tree_kernel, out_shape=jax.ShapeDtypeStruct((LEVELS, 2, K,...  47 us
    unnamed x22, local copies, waits for them, and re-layouts  10.1 us
    all_to_all x1, starting transfers between devices, local(): lax.all_to_all(adj_tests, 'sub', split_axis=1, concat_axis=0, tiled=True)  9.89 us
    pallas_call x1, Pallas kernels, build(): pl.pallas_call(build_kernel, out_shape=(jax.ShapeDtypeStruct((K, 2304), B...  7.33 us
    ppermute x1, starting transfers between devices, local(): om_high = lax.ppermute(omega, 'sub', down)  7.24 us
    ppermute x1, starting transfers between devices, local(): cols_low = lax.ppermute(own_head, 'sub', up)  5.37 us
    ppermute x1, starting transfers between devices, local(): cols_high = lax.ppermute(own_head, 'sub', down)  5.29 us
  transfers between devices with their start and end apart: 5, of which 0 were waited for; matrix products, arithmetic and copies ran while one was open for 5% of the time, Pallas kernels for 7%

profile of v1, /device:TPU:1, one launch (start us, length us, event | category | flops | bytes accessed | tf_op | source)
XLA Modules:
  0.0 97.9 jit_solution(16921659641950048290)
XLA Ops:
  0.0 0.0 copy-start.8
  0.0 0.0 copy-start.7
  0.0 0.8 slice_bitcast_fusion
  0.8 5.4 %collective-permute-start.2 = (s32[96]{0:T(128)S(1)}, s32[96]{0:T(128)S(1)}, u32[]{:S(2)}, u32[]{:S(2)}) collective-permute-start(s32[96]{0:T(128)S(1)} %get-tuple-element.18), channel_id=1, source_target_pairs={{0,1},{1,2},{2,3},{3,4},{4,5},{5,6},{6,7},{7,8},{8,9},{9,10},{10,1... | collective-permute-start | bytes 1160 | tf_op jit(solution)/shard_map/ppermute | solution.py:278
  6.2 5.3 %collective-permute-start.3 = (s32[96]{0:T(128)S(1)}, s32[96]{0:T(128)S(1)}, u32[]{:S(2)}, u32[]{:S(2)}) collective-permute-start(s32[96]{0:T(128)S(1)} %get-tuple-element.18), channel_id=1, source_target_pairs={{1,0},{2,1},{3,2},{4,3},{5,4},{6,5},{7,6},{8,7},{9,8},{10,9},{11,1... | collective-permute-start | bytes 1160 | tf_op jit(solution)/shard_map/ppermute | solution.py:279
  11.5 1.9 %collective-permute-start = (bf16[768,256]{1,0:T(8,128)(2,1)}, bf16[768,256]{1,0:T(8,128)(2,1)}, u32[]{:S(2)}, u32[]{:S(2)}) collective-permute-start(bf16[768,256]{1,0:T(8,128)(2,1)} %om.1), channel_id=1, source_target_pairs={{0,1},{1,2},{2,3},{3,4},{4,5},{5,6},{6,7},{7,8},{8,9},{9,10},{10,1... | collective-permute-start | bytes 1179656 | tf_op jit(solution)/shard_map/ppermute | solution.py:280
  13.4 7.2 %collective-permute-start.1 = (bf16[768,256]{1,0:T(8,128)(2,1)}, bf16[768,256]{1,0:T(8,128)(2,1)}, u32[]{:S(2)}, u32[]{:S(2)}) collective-permute-start(bf16[768,256]{1,0:T(8,128)(2,1)} %om.1), channel_id=1, source_target_pairs={{1,0},{2,1},{3,2},{4,3},{5,4},{6,5},{7,6},{8,7},{9,8},{10,9},{11,1... | collective-permute-start | bytes 1179656 | tf_op jit(solution)/shard_map/ppermute | solution.py:281
  20.7 9.9 %all-to-all-start = ((bf16[4,64,768]{2,0,1:T(4,128)(2,1)}), bf16[4,64,768]{2,0,1:T(4,128)(2,1)}, u32[]{:S(2)}, u32[]{:S(2)}) async-start(bf16[4,64,768]{2,0,1:T(4,128)(2,1)} %bitcast.29), calls=%async_computation | async-start | bytes 786432 | tf_op jit(solution)/shard_map/all_to_all | solution.py:282
  30.6 1.0 %copy.24 = s32[1,9,2,192]{2,3,1,0:T(8,128)S(1)} copy(s32[1,9,2,192]{3,2,1,0:T(2,128)} %param.14) | data formatting | bytes 27648 | tf_op args[6]
  31.6 0.7 broadcast_subtract_fusion
  32.3 0.1 fusion.node_cols
  32.4 0.1 select_reduce_fusion.inv
  32.5 0.0 copy-done.8
  32.6 0.1 slice.11
  32.6 0.9 copy.27
  33.5 0.0 copy-done.7
  33.6 0.9 copy.25
  34.5 0.0 collective-permute-done.2
  34.5 0.0 collective-permute-done.3
  34.5 0.7 copy.26.heads
  35.2 0.0 copy-start.2
  35.2 1.0 copy-done.2
  36.2 0.0 copy-start.3
  36.2 1.0 copy-done.3
  37.2 0.0 copy-start.6
  37.2 0.8 copy-done.6
  38.0 7.3 %build.1 = (bf16[96,2304]{1,0:T(8,128)(2,1)S(1)}, bf16[3,96,768]{2,1,0:T(8,128)(2,1)S(1)}, bf16[2,96,768]{2,1,0:T(8,128)(2,1)S(1)}, bf16[36,96,128]{2,1,0:T(8,12...) custom-call(s32[6,18]{1,0:T(8,128)S(1)} %select_reduce_fusion.inv, ...), custom_call_target="tpu_custom_call" | custom-call | flops 2000000000 | bytes 8000000 | tf_op jit(solution)/shard_map/build/pallas_call | solution.py:76
  45.3 0.0 copy-start
  45.3 0.9 copy-done
  46.2 0.0 copy-start.4
  46.2 0.7 copy-done.4
  46.9 0.0 all-to-all-done
  46.9 1.1 %all_to_all.17.adj = bf16[256,768]{1,0:T(8,128)(2,1)S(1)} reshape(bf16[64,4,768]{2,1,0:T(4,128)(2,1)} %bitcast.1) | data formatting | bytes 786432 | tf_op jit(solution)/shard_map/all_to_all | solution.py:282
  48.0 0.0 collective-permute-done.om_low
  48.0 0.0 collective-permute-done.1.om_high
  48.1 0.0 copy-start.1
  48.1 1.0 %copy-done.1 = bf16[768,256]{1,0:T(8,128)(2,1)S(1)} copy-done((bf16[768,256]{1,0:T(8,128)(2,1)S(1)}, bf16[768,256]{1,0:T(8,128)(2,1)}, u32[]{:S(2)}) %copy-start.1) | copy-done | bytes 393240
  49.1 0.0 copy-start.5
  49.1 1.0 copy-done.5
  50.0 47.0 %tree.1 = bf16[9,2,96,256]{3,2,1,0:T(8,128)(2,1)S(1)} custom-call(bf16[768,256]{1,0:T(8,128)(2,1)} %collective-permute-done.om_low, bf16[768,256]{1,0:T(8,128)(2,1)S(1)} %copy-done.1, bf16[768,256]{1,0:T(8,128)(2,1)} %collective-permute-done.1.om_high, bf16[256,768]{1,0:T(8,128)(2,1)S(1)} %all_to_all.17.adj, bf16[96,2304]{1,0:T(8,128)(2,1)S(1)} %get-tuple-element.11.wf, ...), custom_call_target="tpu_custom_call" | custom-call | tf_op jit(solution)/shard_map/tree/pallas_call | solution.py:243
  97.0 0.9 copy.29
  (2 shorter events, 0.0 us)
Async XLA Ops:
  0.0 32.5 %copy-start.8 = (s32[1,2,768]{2,1,0:T(2,128)S(1)}, s32[1,2,768]{2,1,0:T(2,128)}, u32[]{:S(2)}) copy-start(s32[1,2,768]{2,1,0:T(2,128)} %param.12) | copy-start | bytes 18436
  0.0 33.5 %copy-start.7 = (bf16[1,2,672,96]{2,3,1,0:T(8,128)(2,1)S(1)}, bf16[1,2,672,96]{2,3,1,0:T(8,128)(2,1)}, u32[]{:S(2)}) copy-start(bf16[1,2,672,96]{2,3,1,0:T(8,128)(2,1)} %param.13) | copy-start | bytes 774148
  0.8 33.6 %collective-permute-start.2 = (s32[96]{0:T(128)S(1)}, s32[96]{0:T(128)S(1)}, u32[]{:S(2)}, u32[]{:S(2)}) collective-permute-start(s32[96]{0:T(128)S(1)} %get-tuple-element.18), channel_id=1, source_target_pairs={{0,1},{1,2},{2,3},{3,4},{4,5},{5,6},{6,7},{7,8},{8,9},{9,10},{10,1... | collective-permute-start | bytes 1160 | tf_op jit(solution)/shard_map/ppermute | solution.py:278
  6.2 28.3 %collective-permute-start.3 = (s32[96]{0:T(128)S(1)}, s32[96]{0:T(128)S(1)}, u32[]{:S(2)}, u32[]{:S(2)}) collective-permute-start(s32[96]{0:T(128)S(1)} %get-tuple-element.18), channel_id=1, source_target_pairs={{1,0},{2,1},{3,2},{4,3},{5,4},{6,5},{7,6},{8,7},{9,8},{10,9},{11,1... | collective-permute-start | bytes 1160 | tf_op jit(solution)/shard_map/ppermute | solution.py:279
  11.5 36.5 %collective-permute-start = (bf16[768,256]{1,0:T(8,128)(2,1)}, bf16[768,256]{1,0:T(8,128)(2,1)}, u32[]{:S(2)}, u32[]{:S(2)}) collective-permute-start(bf16[768,256]{1,0:T(8,128)(2,1)} %om.1), channel_id=1, source_target_pairs={{0,1},{1,2},{2,3},{3,4},{4,5},{5,6},{6,7},{7,8},{8,9},{9,10},{10,1... | collective-permute-start | bytes 1179656 | tf_op jit(solution)/shard_map/ppermute | solution.py:280
  13.4 34.6 %collective-permute-start.1 = (bf16[768,256]{1,0:T(8,128)(2,1)}, bf16[768,256]{1,0:T(8,128)(2,1)}, u32[]{:S(2)}, u32[]{:S(2)}) collective-permute-start(bf16[768,256]{1,0:T(8,128)(2,1)} %om.1), channel_id=1, source_target_pairs={{1,0},{2,1},{3,2},{4,3},{5,4},{6,5},{7,6},{8,7},{9,8},{10,9},{11,1... | collective-permute-start | bytes 1179656 | tf_op jit(solution)/shard_map/ppermute | solution.py:281
  20.7 26.3 %all-to-all-start = ((bf16[4,64,768]{2,0,1:T(4,128)(2,1)}), bf16[4,64,768]{2,0,1:T(4,128)(2,1)}, u32[]{:S(2)}, u32[]{:S(2)}) async-start(bf16[4,64,768]{2,0,1:T(4,128)(2,1)} %bitcast.29), calls=%async_computation | async-start | bytes 786432 | tf_op jit(solution)/shard_map/all_to_all | solution.py:282
  35.2 1.0 copy-start.2
  36.2 1.0 copy-start.3
  37.2 0.8 copy-start.6
  45.3 0.9 copy-start
  46.2 0.7 copy-start.4
  48.1 1.0 %copy-start.1 = (bf16[768,256]{1,0:T(8,128)(2,1)S(1)}, bf16[768,256]{1,0:T(8,128)(2,1)}, u32[]{:S(2)}) copy-start(bf16[768,256]{1,0:T(8,128)(2,1)} %om.1) | copy-start | bytes 1179652
  49.1 1.0 copy-start.5

commit v2 on v1

v2 whole, which is shorter than its diff:
```python
import jax
import jax.numpy as jnp
from jax import lax
from jax.experimental import pallas as pl
from jax.experimental.pallas import tpu as pltpu
from jax.sharding import PartitionSpec as P

BF = jnp.bfloat16
F32 = jnp.float32
MESH = pl.DeviceIdType.MESH
K = 96
LEVELS = 9


def mm(a, b):
    return lax.dot_general(a, b, (((1,), (0,)), ((), ())), preferred_element_type=F32)


def mm_nt(a, b):
    return lax.dot_general(a, b, (((1,), (1,)), ((), ())), preferred_element_type=F32)


def mm_tn(a, b):
    return lax.dot_general(a, b, (((0,), (0,)), ((), ())), preferred_element_type=F32)


def onehot(column, width):
    lanes = lax.broadcasted_iota(jnp.int32, (column.shape[0], width), 1).astype(F32)
    return jnp.where(lanes == column, 1.0, 0.0)


def mirror(z):
    return lax.rem(jnp.where(lax.rem(z, 2) == 0, 14 - z, 16 - z), 8)


def flip(v, bit):
    return jnp.where(lax.rem(v // bit, 2) == 0, v + bit, v - bit)


def split(value):
    top = value.astype(BF)
    return top, (value - top.astype(F32)).astype(BF)


def twice(op, top, low):
    return mm(op, top) + mm(op, low)


def kernel(
    tile_cols, omega, tests, near_in, leaf_perms, interp_in, node_perms, maps_in,
    out,
    om, near, lperm, interp, nperm, maps, nrows, lrows, erows, orders, placed, wf, wa, gl, op_s, op_h, op_g,
    adj_in, adj, pan, halo_s, halo_r, s0, r0, hi, lo, rec,
    loc, a2a_s, a2a_r, near_ss, near_rs, halo_ss, halo_rs, ss0, rs0, ss, rs, os_s, os_r,
):
    g = lax.axis_index("grp")
    s = lax.axis_index("sub")
    core = lax.rem(s, 2)
    z = lax.rem(s // 2, 8)
    x = s // 16
    z0 = lax.rem(z, 2)
    left, right = lax.rem(s + 63, 64), lax.rem(s + 1, 64)

    def sub_at(xx, zz, cc):
        return (xx * 8 + zz) * 2 + cc

    mate = sub_at(x, z, 1 - core)
    zmate = sub_at(x, flip(z, 1), core)
    cross = sub_at(x, flip(z, 1), 1 - core)
    partners = [
        {"sub": mate},
        {"sub": zmate},
        {"sub": sub_at(x, flip(z, 2), core)},
        {"sub": sub_at(x, mirror(z), core)},
        {"sub": sub_at(flip(x, 1), z, core)},
        {"sub": sub_at(3 - x, z, core)},
        {"grp": flip(g, 1)},
        {"grp": flip(g, 2)},
        {"grp": mirror(g)},
    ]
    bits = [core] + [lax.rem(z // b, 2) for b in (1, 2, 4)] + [lax.rem(x // b, 2) for b in (1, 2)]
    bits += [lax.rem(g // b, 2) for b in (1, 2, 4)]

    def fetch(src, dst, i):
        copy = pltpu.make_async_copy(src, dst, loc.at[i])
        copy.start()
        return copy

    got_nperm = fetch(node_perms.at[0], nperm, 0)
    got_maps = fetch(maps_in.at[0], maps, 1)
    got_lperm = fetch(leaf_perms.at[0], lperm, 2)
    got_near = fetch(near_in, near, 3)
    got_interp = fetch(interp_in.at[0], interp, 4)
    got_om = fetch(omega, om.at[1], 5)
    own_tests = fetch(tests.at[:, pl.ds(pl.multiple_of(s * 768, 768), 768)], adj_in.at[s], 6)

    barrier = pltpu.get_barrier_semaphore()

    def greet(k, carry):
        pl.semaphore_signal(
            barrier, inc=1, device_id={"sub": lax.rem(s + k, 64)}, device_id_type=MESH
        )
        return carry

    lax.fori_loop(1, 64, greet, 0)
    for who in partners[6:]:
        pl.semaphore_signal(barrier, inc=1, device_id=who, device_id_type=MESH)

    got_nperm.wait()
    nrows[...] = jnp.zeros_like(nrows)
    for j in range(LEVELS):
        nrows[2 * j : 2 * j + 2, 0:192] = nperm[j].astype(F32)
    ncols = nrows[...].T
    ncols = ncols + jnp.where(ncols >= K, 128.0 - K, 0.0)
    got_maps.wait()
    for j in range(LEVELS):
        picks = [onehot(ncols[0:192, 2 * j + i : 2 * j + i + 1], 256) for i in range(2)]
        low_high, high_low = maps[j, 2], maps[j, 3]
        for ch in range(2):
            sel = picks[ch][:K].astype(BF)
            rows = picks[1 - ch]
            full = (rows[:K] + mm_tn(maps[j, 1 - ch], rows[K:].astype(BF))).astype(BF)
            couple = (high_low, low_high) if ch == 0 else (low_high, high_low)
            times = mm if ch == 0 else mm_nt
            for half in range(2):
                at = (j * 2 + ch) * 2 + half
                op_s[at] = sel[:, half * 128 : half * 128 + 128]
                op_g[at] = full[:, half * 128 : half * 128 + 128]
                other = sel[:, (1 - half) * 128 : (1 - half) * 128 + K]
                op_h[at, :, 0:K] = times(other, couple[half]).astype(BF)

    pl.semaphore_wait(barrier, 66)

    started = []

    def send(src, dst, ssem, rsem, who):
        copy = pltpu.make_async_remote_copy(
            src_ref=src, dst_ref=dst, send_sem=ssem, recv_sem=rsem, device_id=who, device_id_type=MESH
        )
        copy.start()
        started.append(copy)
        return copy

    def trade(k):
        peer = lax.rem(s + k, 64)
        return pltpu.make_async_remote_copy(
            src_ref=tests.at[:, pl.ds(pl.multiple_of(peer * 768, 768), 768)],
            dst_ref=adj_in.at[s],
            send_sem=a2a_s.at[peer],
            recv_sem=a2a_r.at[s],
            device_id={"sub": peer},
            device_id_type=MESH,
        )

    got_orders, got_omega = [None, None], [None, None]
    for i, who in ((0, right), (1, left)):
        got_orders[i] = send(leaf_perms.at[0], orders.at[i], near_ss.at[i], near_rs.at[i], {"sub": who})

    def trade_start(k, carry):
        trade(k).start()
        return carry

    lax.fori_loop(1, 64, trade_start, 0)
    for i, who in ((0, right), (1, left)):
        got_omega[i] = send(omega, om.at[2 * i], near_ss.at[2 + i], near_rs.at[2 + i], {"sub": who})

    def cols(which):
        return pl.ds(pl.multiple_of(which * 128, 128), 128)

    got_near.wait()
    base = ((g * 64 + s) - 1) * 6

    def place(q, carry):
        held = [tile_cols[q, t] - base for t in range(12)]
        for m in range(18):
            at = 0
            for t in range(12):
                at = jnp.where(held[t] == m, t + 1, at)
            tile = near[q, jnp.maximum(at - 1, 0)]
            keep = jnp.where(at > 0, 1.0, 0.0)
            placed[pl.ds(pl.multiple_of(q * 128, 128), 128), m * 128 : (m + 1) * 128] = tile * keep.astype(BF)
        return carry

    lax.fori_loop(0, 6, place, 0)
    got_lperm.wait()
    lrows[...] = jnp.zeros_like(lrows)
    lrows[0:2] = lperm[...].astype(F32)
    lcols = lrows[...].T
    wf[...] = mm(onehot(lcols[0:K, 0:1], 768).astype(BF), placed[...]).astype(BF)
    got_interp.wait()
    for i in range(2):
        tail = onehot(lcols[K:768, i : i + 1], 768).astype(BF)
        gl[i] = (onehot(lcols[0:K, i : i + 1], 768) + mm(interp[i], tail)).astype(BF)
    erows[...] = jnp.zeros_like(erows)
    for i in range(2):
        got_orders[i].wait_recv()
        erows[i : i + 1] = orders[i, 1:2, 0:128].astype(F32)
    ecols = erows[...].T
    for k, col in enumerate((ecols[0:K, 0:1], lcols[0:K, 1:2], ecols[0:K, 1:2])):
        wa[k] = mm_nt(onehot(col, 768).astype(BF), placed[:, k * 768 : (k + 1) * 768]).astype(BF)

    firsts = [None] * 4

    def first(q):
        s0[q] = pan[q, :, cols(1 - core)].astype(BF)
        firsts[q] = send(s0.at[q], r0.at[q], ss0.at[q], rs0.at[q], {"sub": mate})

    got_om.wait()
    pan[1] = mm(gl[1], om[1])
    first(1)
    total = mm(wf[:, 768:1536], om[1])
    for i in range(2):
        got_omega[i].wait_recv()
        total = total + mm(wf[:, i * 1536 : i * 1536 + 768], om[2 * i])
    pan[0] = total
    first(0)

    own_tests.wait()

    def trade_wait(k, carry):
        peer = lax.rem(s + k, 64)
        pltpu.make_async_remote_copy(
            src_ref=adj_in.at[peer],
            dst_ref=adj_in.at[peer],
            send_sem=a2a_s.at[peer],
            recv_sem=a2a_r.at[peer],
            device_id={"sub": peer},
            device_id_type=MESH,
        ).wait_recv()
        return carry

    lax.fori_loop(1, 64, trade_wait, 0)
    adj[...] = adj_in[...].reshape(256, 768)
    halos = []
    for i, k, who in ((0, 0, left), (1, 2, right)):
        halo_s[i] = mm_nt(wa[k], adj[...]).astype(BF)
        halos.append(send(halo_s.at[i], halo_r.at[i], halo_ss.at[i], halo_rs.at[i], {"sub": who}))
    pan[3] = mm_nt(gl[0], adj[...])
    first(3)
    own_adj = mm_nt(wa[1], adj[...])
    for copy in halos:
        copy.wait_recv()
    pan[2] = own_adj + halo_r[0].astype(F32) + halo_r[1].astype(F32)
    first(2)

    for ch in range(2):
        f_top, f_low = split(pan[2 * ch, :, cols(core)])
        o_top, o_low = split(pan[2 * ch + 1, :, cols(core)])
        own, far = ch * 2 + core, ch * 2 + 1 - core
        firsts[2 * ch + 1].wait_recv()
        o_far = r0[2 * ch + 1]
        o_new = twice(op_g[own][:, :K], o_top, o_low) + mm(op_g[far][:, :K], o_far)
        hi[0, 2 * ch + 1], lo[2 * ch + 1] = split(o_new)
        f_new = twice(op_s[own][:, :K], f_top, f_low) - twice(op_h[own][:, :K], o_top, o_low)
        f_new = f_new - mm(op_h[far][:, :K], o_far)
        firsts[2 * ch].wait_recv()
        f_new = f_new + mm(op_s[far][:, :K], r0[2 * ch])
        hi[0, 2 * ch], lo[2 * ch] = split(f_new)

    ways = []
    arrivals = []
    for i in (1, 0):
        ways.append(send(hi.at[0, 2 * (1 - z0) + i], rec.at[0, i], ss.at[0, i], rs.at[0, i], partners[1]))
    ways = [ways[1], ways[0]]
    for ch in range(2):
        out[0, ch, :, cols(core)] = hi[0, 2 * ch]
        arrivals.append(
            send(hi.at[0, 2 * ch], out.at[0, ch, :, cols(core)], os_s.at[0, ch], os_r.at[0, ch], partners[0])
        )
    f_top, o_top = hi[0, 2 * z0], hi[0, 2 * z0 + 1]
    f_low, o_low = lo[2 * z0], lo[2 * z0 + 1]
    peers = ({"sub": mate}, {"sub": zmate}, {"sub": cross})
    for j in range(1, LEVELS):
        base = (j * 2 + z0) * 2
        own, far = base + bits[j], base + 1 - bits[j]
        last = j == LEVELS - 1
        o_part = None if last else twice(op_g[own][:, :K], o_top, o_low)
        f_part = twice(op_s[own][:, :K], f_top, f_low) - twice(op_h[own][:, :K], o_top, o_low)
        ways[1].wait_recv()
        o_far = rec[j - 1, 1]
        nexts = [None, None]
        if not last:
            o_top, o_low = split(o_part + mm(op_g[far][:, :K], o_far))
            hi[j, 1] = o_top
            nexts[1] = send(hi.at[j, 1], rec.at[j, 1], ss.at[j, 1], rs.at[j, 1], partners[j + 1])
        f_part = f_part - mm(op_h[far][:, :K], o_far)
        ways[0].wait_recv()
        f_top, f_low = split(f_part + mm(op_s[far][:, :K], rec[j - 1, 0]))
        hi[j, 0] = f_top
        if not last:
            nexts[0] = send(hi.at[j, 0], rec.at[j, 0], ss.at[j, 0], rs.at[j, 0], partners[j + 1])
        for k, who in enumerate(peers):
            arrivals.append(
                send(hi.at[j, 0], out.at[j, z0, :, cols(core)], os_s.at[j, k], os_r.at[j, k], who)
            )
        out[j, z0, :, cols(core)] = f_top
        ways = nexts
    for copy in arrivals:
        copy.wait_recv()
    for copy in started:
        copy.wait_send()

    def trade_end(k, carry):
        trade(k).wait_send()
        return carry

    lax.fori_loop(1, 64, trade_end, 0)


def local(omega, adj_tests, near_tiles, tile_cols, leaf_perms, leaf_interp, node_perms, node_maps):
    dma = pltpu.SemaphoreType.DMA
    anywhere = pl.BlockSpec(memory_space=pl.ANY)
    ops = pltpu.VMEM((LEVELS * 4, K, 128), BF)
    return pl.pallas_call(
        kernel,
        out_shape=jax.ShapeDtypeStruct((LEVELS, 2, K, 256), BF),
        in_specs=[pl.BlockSpec(memory_space=pltpu.SMEM)] + [anywhere] * 7,
        out_specs=pl.BlockSpec(memory_space=pltpu.VMEM),
        scratch_shapes=[
            pltpu.VMEM((3, 768, 256), BF),
            pltpu.VMEM((6, 12, 128, 128), BF),
            pltpu.VMEM((2, 768), jnp.int32),
            pltpu.VMEM((2, K, 672), BF),
            pltpu.VMEM((LEVELS, 2, 192), jnp.int32),
            pltpu.VMEM((LEVELS, 4, K, K), BF),
            pltpu.VMEM((24, 256), F32),
            pltpu.VMEM((8, 768), F32),
            pltpu.VMEM((8, 128), F32),
            pltpu.VMEM((2, 2, 768), jnp.int32),
            pltpu.VMEM((768, 2304), BF),
            pltpu.VMEM((K, 2304), BF),
            pltpu.VMEM((3, K, 768), BF),
            pltpu.VMEM((2, K, 768), BF),
            ops,
            ops,
            ops,
            pltpu.VMEM((64, 4, 768), BF),
            pltpu.VMEM((256, 768), BF),
            pltpu.VMEM((4, K, 256), F32),
            pltpu.VMEM((2, K, 256), BF),
            pltpu.VMEM((2, K, 256), BF),
            pltpu.VMEM((4, K, 128), BF),
            pltpu.VMEM((4, K, 128), BF),
            pltpu.VMEM((LEVELS, 4, K, 128), BF),
            pltpu.VMEM((4, K, 128), BF),
            pltpu.VMEM((LEVELS - 1, 2, K, 128), BF),
            dma((7,)),
            dma((64,)),
            dma((64,)),
            dma((4,)),
            dma((4,)),
            dma((2,)),
            dma((2,)),
            dma((4,)),
            dma((4,)),
            dma((LEVELS, 2)),
            dma((LEVELS, 2)),
            dma((LEVELS, 3)),
            dma((LEVELS, 3)),
        ],
        compiler_params=pltpu.CompilerParams(
            collective_id=0, has_side_effects=True, vmem_limit_bytes=56 << 20
        ),
        name="window",
    )(
        tile_cols,
        omega,
        adj_tests,
        near_tiles,
        leaf_perms,
        jnp.swapaxes(leaf_interp, 2, 3),
        node_perms,
        node_maps,
    )[None]


def solution(mesh):
    placed = (
        P(("grp", "sub"), None),
        P("sub", "grp"),
        P(("grp", "sub"), None, None, None),
        P(("grp", "sub"), None),
        P(("grp", "sub"), None, None),
        P(("grp", "sub"), None, None, None),
        P(("grp", "sub"), None, None, None),
        P(("grp", "sub"), None, None, None, None),
    )
    return jax.shard_map(
        local,
        mesh=mesh,
        in_specs=placed,
        out_specs=P(("grp", "sub"), None, None, None, None),
        check_vma=False,
    )
```

time: 98.6 us -> 75.1 us (0.76)
  starting transfers between devices: 29.7 us -> 0 us
  Pallas kernels: 54.3 us -> 72.8 us
  local copies, waits for them, and re-layouts: 12.8 us -> 2.14 us
    ppermute x4 -> x0, starting transfers between devices: 19.8 us -> none  [the longest x1 7.24 us: local(): om_high = lax.ppermute(omega, 'sub', down)]
    pallas_call x2 -> x1, Pallas kernels: 54.3 us -> 72.8 us  [local(): pl.pallas_call(kernel, out_shape=jax.ShapeDtypeStruct((LEVELS, 2, K, 256)...]
    all_to_all x1 -> x0, starting transfers between devices: 9.89 us -> none  [local(): lax.all_to_all(adj_tests, 'sub', split_axis=1, concat_axis=0, tiled=True)]
    unnamed x22 -> x1, local copies, waits for them, and re-layouts: 10.1 us -> 2.14 us
    another operation x2 -> x0, local copies, waits for them, and re-layouts: 1.55 us -> none  [local(): jnp.stack([leaf_perms[0, 0, :K], own_head, cols_low, cols_high], axis=1)]
    all_to_all x1 -> x0, local copies, waits for them, and re-layouts: 1.09 us -> none  [local(): lax.all_to_all(adj_tests, 'sub', split_axis=1, concat_axis=0, tiled=True)]
  transfers between devices with their start and end apart: 5 -> 0, of which waited for: 0 -> 0; matrix products, arithmetic and copies ran while one was open for 5% -> 0% of each run, Pallas kernels for 7% -> 0%
where the time goes in v2:
time: 75.1 us; the launch traced here: 74.9 us
  Pallas kernels  72.8 us (97%)
  local copies, waits for them, and re-layouts  2.14 us (3%)
    pallas_call x1, Pallas kernels, local(): pl.pallas_call(kernel, out_shape=jax.ShapeDtypeStruct((LEVELS, 2, K, 256)...  72.8 us
    unnamed x1, local copies, waits for them, and re-layouts  2.14 us

profile of v2, /device:TPU:1, one launch (start us, length us, event | category | flops | bytes accessed | tf_op | source)
XLA Modules:
  0.0 74.9 jit_solution(14657696084145594079)
XLA Ops:
  0.0 72.8 %window.1 = bf16[9,2,96,256]{3,2,1,0:T(8,128)(2,1)} custom-call(s32[6,12]{1,0:T(8,128)} %tile_cols.1, bf16[768,256]{1,0:T(8,128)(2,1)} %omega.1, bf16[4,49152]{1,0:T(4,128)(2,1)} %tests.1, bf16[6,12,128,128]{3,2,1,0:T(8,128)(2,1)} %near_in.1, s32[1,2,768]{2,1,0:T(2,128)} %leaf_perms.1, bf16[1,2,96,672]{3,2,1,0:T(8,128)(2,1)} %bitcast.3, ...), custom_call_target="tpu_custom_call" | custom-call | tf_op jit(solution)/shard_map/window/pallas_call | solution.py:314
  72.8 2.1 %copy.10 = bf16[1,9,2,96,256]{4,3,2,1,0:T(8,128)(2,1)} copy(bf16[1,9,2,96,256]{4,3,2,1,0:T(8,128)(2,1)} %bitcast.2) | data formatting | bytes 1769472

commit v3 on v2

--- a/solution.py
+++ b/solution.py
@@ -49,9 +49,9 @@
 def kernel(
     tile_cols, omega, tests, near_in, leaf_perms, interp_in, node_perms, maps_in,
     out,
-    om, near, lperm, interp, nperm, maps, nrows, lrows, erows, orders, placed, wf, wa, gl, op_s, op_h, op_g,
-    adj_in, adj, pan, halo_s, halo_r, s0, r0, hi, lo, rec,
-    loc, a2a_s, a2a_r, near_ss, near_rs, halo_ss, halo_rs, ss0, rs0, ss, rs, os_s, os_r,
+    om, om_mate, w_in, near, lperm, interp, nperm, maps, nrows, lrows, erows, orders, placed, wf, wa, gl, op_s, op_h, op_g,
+    adj_in, adj, pan, pan_far, d_s, d_r, s0, r0, hi, lo, rec,
+    loc, a2a_s, a2a_r, near_ss, near_rs, d_ss, d_rs, ss0, rs0, ss, rs, os_s, os_r,
 ):
     g = lax.axis_index("grp")
     s = lax.axis_index("sub")
@@ -60,6 +60,8 @@
     x = s // 16
     z0 = lax.rem(z, 2)
     left, right = lax.rem(s + 63, 64), lax.rem(s + 1, 64)
+    outer = lax.rem(s + 63 + 2 * core, 64)
+    outer_twin = lax.rem(s + 62 + 4 * core, 64)
 
     def sub_at(xx, zz, cc):
         return (xx * 8 + zz) * 2 + cc
@@ -91,7 +93,7 @@
     got_lperm = fetch(leaf_perms.at[0], lperm, 2)
     got_near = fetch(near_in, near, 3)
     got_interp = fetch(interp_in.at[0], interp, 4)
-    got_om = fetch(omega, om.at[1], 5)
+    got_om = fetch(omega, om, 5)
     own_tests = fetch(tests.at[:, pl.ds(pl.multiple_of(s * 768, 768), 768)], adj_in.at[s], 6)
 
     barrier = pltpu.get_barrier_semaphore()
@@ -146,29 +148,32 @@
         return pltpu.make_async_remote_copy(
             src_ref=tests.at[:, pl.ds(pl.multiple_of(peer * 768, 768), 768)],
             dst_ref=adj_in.at[s],
-            send_sem=a2a_s.at[peer],
-            recv_sem=a2a_r.at[s],
+            send_sem=a2a_s,
+            recv_sem=a2a_r,
             device_id={"sub": peer},
             device_id_type=MESH,
         )
 
-    got_orders, got_omega = [None, None], [None, None]
+    got_orders = [None, None]
     for i, who in ((0, right), (1, left)):
         got_orders[i] = send(leaf_perms.at[0], orders.at[i], near_ss.at[i], near_rs.at[i], {"sub": who})
+    got_mate = send(omega, om_mate, near_ss.at[2], near_rs.at[2], {"sub": mate})
 
     def trade_start(k, carry):
         trade(k).start()
         return carry
 
     lax.fori_loop(1, 64, trade_start, 0)
-    for i, who in ((0, right), (1, left)):
-        got_omega[i] = send(omega, om.at[2 * i], near_ss.at[2 + i], near_rs.at[2 + i], {"sub": who})
 
     def cols(which):
         return pl.ds(pl.multiple_of(which * 128, 128), 128)
 
+    got_lperm.wait()
+    lrows[...] = jnp.zeros_like(lrows)
+    lrows[0:2] = lperm[...].astype(F32)
+    lcols = lrows[...].T
+    base = ((g * 64 + s) - 1) * 6
     got_near.wait()
-    base = ((g * 64 + s) - 1) * 6
 
     def place(q, carry):
         held = [tile_cols[q, t] - base for t in range(12)]
@@ -182,15 +187,48 @@
         return carry
 
     lax.fori_loop(0, 6, place, 0)
-    got_lperm.wait()
-    lrows[...] = jnp.zeros_like(lrows)
-    lrows[0:2] = lperm[...].astype(F32)
-    lcols = lrows[...].T
-    wf[...] = mm(onehot(lcols[0:K, 0:1], 768).astype(BF), placed[...]).astype(BF)
+    picked = onehot(lcols[0:K, 0:1], 768).astype(BF)
+    for k in range(3):
+        wf[k] = mm(picked, placed[:, k * 768 : (k + 1) * 768]).astype(BF)
+    got_w = send(wf.at[2 * core], w_in, near_ss.at[3], near_rs.at[3], {"sub": outer})
+
+    firsts = [None] * 5
+
+    def first(q, value):
+        s0[q] = value.astype(BF)
+        firsts[q] = send(s0.at[q], r0.at[q], ss0.at[q], rs0.at[q], {"sub": mate})
+
+    def outward(i, value):
+        for half in range(2):
+            d_s[i, half] = value[:, half * 128 : half * 128 + 128].astype(BF)
+        copies = []
+        for n, (half, who) in enumerate(((1 - core, outer), (core, outer_twin))):
+            copies.append(
+                send(d_s.at[i, half], d_r.at[i, 1 - core], d_ss.at[i, n], d_rs.at[i, 1 - core], {"sub": who})
+            )
+        return copies
+
+    def outward_done(i):
+        for slot in range(2):
+            pltpu.make_async_remote_copy(
+                src_ref=d_s.at[i, slot],
+                dst_ref=d_r.at[i, slot],
+                send_sem=d_ss.at[i, slot],
+                recv_sem=d_rs.at[i, slot],
+                device_id={"sub": outer},
+                device_id_type=MESH,
+            ).wait_recv()
+
     got_interp.wait()
-    for i in range(2):
+    for i in (1, 0):
         tail = onehot(lcols[K:768, i : i + 1], 768).astype(BF)
         gl[i] = (onehot(lcols[0:K, i : i + 1], 768) + mm(interp[i], tail)).astype(BF)
+    got_om.wait()
+    pan[1] = mm(gl[1], om[...])
+    first(1, pan[1, :, cols(1 - core)])
+    got_mate.wait_recv()
+    pan[0] = mm(wf[1], om[...]) + mm(wf[2 * (1 - core)], om_mate[...])
+    first(0, pan[0, :, cols(1 - core)])
     erows[...] = jnp.zeros_like(erows)
     for i in range(2):
         got_orders[i].wait_recv()
@@ -198,75 +236,87 @@
     ecols = erows[...].T
     for k, col in enumerate((ecols[0:K, 0:1], lcols[0:K, 1:2], ecols[0:K, 1:2])):
         wa[k] = mm_nt(onehot(col, 768).astype(BF), placed[:, k * 768 : (k + 1) * 768]).astype(BF)
-
-    firsts = [None] * 4
-
-    def first(q):
-        s0[q] = pan[q, :, cols(1 - core)].astype(BF)
-        firsts[q] = send(s0.at[q], r0.at[q], ss0.at[q], rs0.at[q], {"sub": mate})
-
-    got_om.wait()
-    pan[1] = mm(gl[1], om[1])
-    first(1)
-    total = mm(wf[:, 768:1536], om[1])
-    for i in range(2):
-        got_omega[i].wait_recv()
-        total = total + mm(wf[:, i * 1536 : i * 1536 + 768], om[2 * i])
-    pan[0] = total
-    first(0)
-
-    own_tests.wait()
-
-    def trade_wait(k, carry):
-        peer = lax.rem(s + k, 64)
-        pltpu.make_async_remote_copy(
-            src_ref=adj_in.at[peer],
-            dst_ref=adj_in.at[peer],
-            send_sem=a2a_s.at[peer],
-            recv_sem=a2a_r.at[peer],
-            device_id={"sub": peer},
+    got_w.wait_recv()
+    outward(0, mm(w_in[...], om[...]))
+
+    def chain_send(ch, i):
+        return pltpu.make_async_remote_copy(
+            src_ref=hi.at[0, 2 * ch + i],
+            dst_ref=rec.at[0, i],
+            send_sem=ss.at[0, i],
+            recv_sem=rs.at[0, i],
+            device_id=partners[1],
             device_id_type=MESH,
-        ).wait_recv()
-        return carry
-
-    lax.fori_loop(1, 64, trade_wait, 0)
-    adj[...] = adj_in[...].reshape(256, 768)
-    halos = []
-    for i, k, who in ((0, 0, left), (1, 2, right)):
-        halo_s[i] = mm_nt(wa[k], adj[...]).astype(BF)
-        halos.append(send(halo_s.at[i], halo_r.at[i], halo_ss.at[i], halo_rs.at[i], {"sub": who}))
-    pan[3] = mm_nt(gl[0], adj[...])
-    first(3)
-    own_adj = mm_nt(wa[1], adj[...])
-    for copy in halos:
-        copy.wait_recv()
-    pan[2] = own_adj + halo_r[0].astype(F32) + halo_r[1].astype(F32)
-    first(2)
-
-    for ch in range(2):
-        f_top, f_low = split(pan[2 * ch, :, cols(core)])
-        o_top, o_low = split(pan[2 * ch + 1, :, cols(core)])
+        )
+
+    def chain_start(ch, i):
+        @pl.when(z0 == 1 - ch)
+        def _():
+            chain_send(ch, i).start()
+
+    def tests_up(ch):
         own, far = ch * 2 + core, ch * 2 + 1 - core
-        firsts[2 * ch + 1].wait_recv()
-        o_far = r0[2 * ch + 1]
-        o_new = twice(op_g[own][:, :K], o_top, o_low) + mm(op_g[far][:, :K], o_far)
-        hi[0, 2 * ch + 1], lo[2 * ch + 1] = split(o_new)
-        f_new = twice(op_s[own][:, :K], f_top, f_low) - twice(op_h[own][:, :K], o_top, o_low)
-        f_new = f_new - mm(op_h[far][:, :K], o_far)
-        firsts[2 * ch].wait_recv()
-        f_new = f_new + mm(op_s[far][:, :K], r0[2 * ch])
-        hi[0, 2 * ch], lo[2 * ch] = split(f_new)
-
-    ways = []
-    arrivals = []
-    for i in (1, 0):
-        ways.append(send(hi.at[0, 2 * (1 - z0) + i], rec.at[0, i], ss.at[0, i], rs.at[0, i], partners[1]))
-    ways = [ways[1], ways[0]]
-    for ch in range(2):
-        out[0, ch, :, cols(core)] = hi[0, 2 * ch]
+        q = 2 * ch + 1
+        top, low = split(pan[q, :, cols(core)])
+        firsts[q].wait_recv()
+        top_new, lo[q] = split(twice(op_g[own][:, :K], top, low) + mm(op_g[far][:, :K], r0[q]))
+        hi[0, q] = top_new
+        chain_start(ch, 1)
+        return twice(op_h[own][:, :K], top, low) + mm(op_h[far][:, :K], r0[q])
+
+    def rows_up(ch, coupled, own_rows, far_rows):
+        own, far = ch * 2 + core, ch * 2 + 1 - core
+        new = twice(op_s[own][:, :K], *split(own_rows)) + twice(op_s[far][:, :K], *split(far_rows)) - coupled
+        top_new, lo[2 * ch] = split(new)
+        hi[0, 2 * ch] = top_new
+        chain_start(ch, 0)
+        out[0, ch, :, cols(core)] = top_new
         arrivals.append(
             send(hi.at[0, 2 * ch], out.at[0, ch, :, cols(core)], os_s.at[0, ch], os_r.at[0, ch], partners[0])
         )
+
+    arrivals = []
+    coupled_fwd = tests_up(0)
+
+    own_tests.wait()
+    everyone = adj_in.at[pl.ds(0, 63)]
+    trades = pltpu.make_async_remote_copy(
+        src_ref=everyone,
+        dst_ref=everyone,
+        send_sem=a2a_s,
+        recv_sem=a2a_r,
+        device_id={"sub": right},
+        device_id_type=MESH,
+    )
+    trades.wait_recv()
+    adj[...] = adj_in[...].reshape(256, 768)
+    outward(1, mm_nt(wa[2 * core], adj[...]))
+    pan[3] = mm_nt(gl[0], adj[...])
+    first(3, pan[3, :, cols(1 - core)])
+    pan[2] = mm_nt(wa[1], adj[...])
+    first(4, pan[2, :, cols(1 - core)])
+    pan_far[...] = mm_nt(wa[2 * (1 - core)], adj[...])
+    first(2, pan_far[:, cols(1 - core)])
+    firsts[0].wait_recv()
+    outward_done(0)
+    rows_up(
+        0,
+        coupled_fwd,
+        pan[0, :, cols(core)] + d_r[0, core].astype(F32),
+        r0[0].astype(F32) + d_r[0, 1 - core].astype(F32),
+    )
+    coupled_adj = tests_up(1)
+    firsts[2].wait_recv()
+    firsts[4].wait_recv()
+    outward_done(1)
+    rows_up(
+        1,
+        coupled_adj,
+        pan[2, :, cols(core)] + r0[2].astype(F32) + d_r[1, core].astype(F32),
+        pan_far[:, cols(core)] + r0[4].astype(F32) + d_r[1, 1 - core].astype(F32),
+    )
+    ways = [chain_send(0, 0), chain_send(0, 1)]
+    started += ways
     f_top, o_top = hi[0, 2 * z0], hi[0, 2 * z0 + 1]
     f_low, o_low = lo[2 * z0], lo[2 * z0 + 1]
     peers = ({"sub": mate}, {"sub": zmate}, {"sub": cross})
@@ -300,11 +350,7 @@
     for copy in started:
         copy.wait_send()
 
-    def trade_end(k, carry):
-        trade(k).wait_send()
-        return carry
-
-    lax.fori_loop(1, 64, trade_end, 0)
+    trades.wait_send()
 
 
 def local(omega, adj_tests, near_tiles, tile_cols, leaf_perms, leaf_interp, node_perms, node_maps):
@@ -317,7 +363,9 @@
         in_specs=[pl.BlockSpec(memory_space=pltpu.SMEM)] + [anywhere] * 7,
         out_specs=pl.BlockSpec(memory_space=pltpu.VMEM),
         scratch_shapes=[
-            pltpu.VMEM((3, 768, 256), BF),
+            pltpu.VMEM((768, 256), BF),
+            pltpu.VMEM((768, 256), BF),
+            pltpu.VMEM((K, 768), BF),
             pltpu.VMEM((6, 12, 128, 128), BF),
             pltpu.VMEM((2, 768), jnp.int32),
             pltpu.VMEM((2, K, 672), BF),
@@ -328,7 +376,7 @@
             pltpu.VMEM((8, 128), F32),
             pltpu.VMEM((2, 2, 768), jnp.int32),
             pltpu.VMEM((768, 2304), BF),
-            pltpu.VMEM((K, 2304), BF),
+            pltpu.VMEM((3, K, 768), BF),
             pltpu.VMEM((3, K, 768), BF),
             pltpu.VMEM((2, K, 768), BF),
             ops,
@@ -337,22 +385,23 @@
             pltpu.VMEM((64, 4, 768), BF),
             pltpu.VMEM((256, 768), BF),
             pltpu.VMEM((4, K, 256), F32),
-            pltpu.VMEM((2, K, 256), BF),
-            pltpu.VMEM((2, K, 256), BF),
-            pltpu.VMEM((4, K, 128), BF),
-            pltpu.VMEM((4, K, 128), BF),
+            pltpu.VMEM((K, 256), F32),
+            pltpu.VMEM((2, 2, K, 128), BF),
+            pltpu.VMEM((2, 2, K, 128), BF),
+            pltpu.VMEM((5, K, 128), BF),
+            pltpu.VMEM((5, K, 128), BF),
             pltpu.VMEM((LEVELS, 4, K, 128), BF),
             pltpu.VMEM((4, K, 128), BF),
             pltpu.VMEM((LEVELS - 1, 2, K, 128), BF),
             dma((7,)),
-            dma((64,)),
-            dma((64,)),
+            dma,
+            dma,
             dma((4,)),
             dma((4,)),
-            dma((2,)),
-            dma((2,)),
-            dma((4,)),
-            dma((4,)),
+            dma((2, 2)),
+            dma((2, 2)),
+            dma((5,)),
+            dma((5,)),
             dma((LEVELS, 2)),
             dma((LEVELS, 2)),
             dma((LEVELS, 3)),

time: 75.1 us -> 68.4 us (0.911)
  Pallas kernels: 72.8 us -> 66.1 us
    pallas_call x1, Pallas kernels: 72.8 us -> 66.1 us  [local(): pl.pallas_call(kernel, out_shape=jax.ShapeDtypeStruct((LEVELS, 2, K, 256)...]
where the time goes in v3:
time: 68.4 us; the launch traced here: 68.2 us
  Pallas kernels  66.1 us (97%)
  local copies, waits for them, and re-layouts  2.14 us (3%)
    pallas_call x1, Pallas kernels, local(): pl.pallas_call(kernel, out_shape=jax.ShapeDtypeStruct((LEVELS, 2, K, 256)...  66.1 us
    unnamed x1, local copies, waits for them, and re-layouts  2.14 us

profile of v3, /device:TPU:1, one launch (start us, length us, event | category | flops | bytes accessed | tf_op | source)
XLA Modules:
  0.0 68.2 jit_solution(6534562628858615005)
XLA Ops:
  0.0 66.1 %window.1 = bf16[9,2,96,256]{3,2,1,0:T(8,128)(2,1)} custom-call(s32[6,12]{1,0:T(8,128)} %tile_cols.1, bf16[768,256]{1,0:T(8,128)(2,1)} %omega.1, bf16[4,49152]{1,0:T(4,128)(2,1)} %tests.1, bf16[6,12,128,128]{3,2,1,0:T(8,128)(2,1)} %near_in.1, s32[1,2,768]{2,1,0:T(2,128)} %leaf_perms.1, bf16[1,2,96,672]{3,2,1,0:T(8,128)(2,1)} %bitcast.3, ...), custom_call_target="tpu_custom_call" | custom-call | tf_op jit(solution)/shard_map/window/pallas_call | solution.py:360
  66.1 2.1 %copy.10 = bf16[1,9,2,96,256]{4,3,2,1,0:T(8,128)(2,1)} copy(bf16[1,9,2,96,256]{4,3,2,1,0:T(8,128)(2,1)} %bitcast.2) | data formatting | bytes 1769472

commit v4 on v3

--- a/solution.py
+++ b/solution.py
@@ -50,8 +50,8 @@
     tile_cols, omega, tests, near_in, leaf_perms, interp_in, node_perms, maps_in,
     out,
     om, om_mate, w_in, near, lperm, interp, nperm, maps, nrows, lrows, erows, orders, placed, wf, wa, gl, op_s, op_h, op_g,
-    adj_in, adj, pan, pan_far, d_s, d_r, s0, r0, hi, lo, rec,
-    loc, a2a_s, a2a_r, near_ss, near_rs, d_ss, d_rs, ss0, rs0, ss, rs, os_s, os_r,
+    adj_in, adj, pan, pan_far, d_s, d_r, s0, r0, hi, lo, rec, fin_s, fin_r,
+    loc, a2a_s, a2a_r, near_ss, near_rs, d_ss, d_rs, ss0, rs0, ss, rs, os_s, os_r, fin_ss, fin_rs,
 ):
     g = lax.axis_index("grp")
     s = lax.axis_index("sub")
@@ -79,6 +79,7 @@
         {"grp": flip(g, 1)},
         {"grp": flip(g, 2)},
         {"grp": mirror(g)},
+        {"grp": jnp.where(lax.rem(g // 2, 2) == 0, 5 - g, 9 - g)},
     ]
     bits = [core] + [lax.rem(z // b, 2) for b in (1, 2, 4)] + [lax.rem(x // b, 2) for b in (1, 2)]
     bits += [lax.rem(g // b, 2) for b in (1, 2, 4)]
@@ -131,7 +132,7 @@
                 other = sel[:, (1 - half) * 128 : (1 - half) * 128 + K]
                 op_h[at, :, 0:K] = times(other, couple[half]).astype(BF)
 
-    pl.semaphore_wait(barrier, 66)
+    pl.semaphore_wait(barrier, 67)
 
     started = []
 
@@ -221,8 +222,9 @@
 
     got_interp.wait()
     for i in (1, 0):
+        into = gl if i == 1 else wa
         tail = onehot(lcols[K:768, i : i + 1], 768).astype(BF)
-        gl[i] = (onehot(lcols[0:K, i : i + 1], 768) + mm(interp[i], tail)).astype(BF)
+        into[1] = (onehot(lcols[0:K, i : i + 1], 768) + mm(interp[i], tail)).astype(BF)
     got_om.wait()
     pan[1] = mm(gl[1], om[...])
     first(1, pan[1, :, cols(1 - core)])
@@ -235,7 +237,8 @@
         erows[i : i + 1] = orders[i, 1:2, 0:128].astype(F32)
     ecols = erows[...].T
     for k, col in enumerate((ecols[0:K, 0:1], lcols[0:K, 1:2], ecols[0:K, 1:2])):
-        wa[k] = mm_nt(onehot(col, 768).astype(BF), placed[:, k * 768 : (k + 1) * 768]).astype(BF)
+        at = (3 * core, 2, 3 * (1 - core))[k]
+        wa[at] = mm_nt(onehot(col, 768).astype(BF), placed[:, k * 768 : (k + 1) * 768]).astype(BF)
     got_w.wait_recv()
     outward(0, mm(w_in[...], om[...]))
 
@@ -290,12 +293,13 @@
     )
     trades.wait_recv()
     adj[...] = adj_in[...].reshape(256, 768)
-    outward(1, mm_nt(wa[2 * core], adj[...]))
-    pan[3] = mm_nt(gl[0], adj[...])
+    outward(1, mm_nt(wa[0], adj[...]))
+    inner = mm_nt(wa[1:4].reshape(3 * K, 768), adj[...])
+    pan[3] = inner[0:K]
+    pan[2] = inner[K : 2 * K]
+    pan_far[...] = inner[2 * K :]
     first(3, pan[3, :, cols(1 - core)])
-    pan[2] = mm_nt(wa[1], adj[...])
     first(4, pan[2, :, cols(1 - core)])
-    pan_far[...] = mm_nt(wa[2 * (1 - core)], adj[...])
     first(2, pan_far[:, cols(1 - core)])
     firsts[0].wait_recv()
     outward_done(0)
@@ -320,31 +324,59 @@
     f_top, o_top = hi[0, 2 * z0], hi[0, 2 * z0 + 1]
     f_low, o_low = lo[2 * z0], lo[2 * z0 + 1]
     peers = ({"sub": mate}, {"sub": zmate}, {"sub": cross})
-    for j in range(1, LEVELS):
+    def publish(j, top=None):
+        if top is not None:
+            hi[j, 0] = top
+            out[j, z0, :, cols(core)] = top
+        for k, who in enumerate(peers):
+            arrivals.append(
+                send(hi.at[j, 0], out.at[j, z0, :, cols(core)], os_s.at[j, k], os_r.at[j, k], who)
+            )
+
+    last = LEVELS - 3
+    for j in range(1, last + 1):
         base = (j * 2 + z0) * 2
         own, far = base + bits[j], base + 1 - bits[j]
-        last = j == LEVELS - 1
-        o_part = None if last else twice(op_g[own][:, :K], o_top, o_low)
+        o_part = twice(op_g[own][:, :K], o_top, o_low)
         f_part = twice(op_s[own][:, :K], f_top, f_low) - twice(op_h[own][:, :K], o_top, o_low)
         ways[1].wait_recv()
         o_far = rec[j - 1, 1]
         nexts = [None, None]
-        if not last:
-            o_top, o_low = split(o_part + mm(op_g[far][:, :K], o_far))
+        o_top, o_low = split(o_part + mm(op_g[far][:, :K], o_far))
+        if j < last:
             hi[j, 1] = o_top
             nexts[1] = send(hi.at[j, 1], rec.at[j, 1], ss.at[j, 1], rs.at[j, 1], partners[j + 1])
         f_part = f_part - mm(op_h[far][:, :K], o_far)
         ways[0].wait_recv()
         f_top, f_low = split(f_part + mm(op_s[far][:, :K], rec[j - 1, 0]))
-        hi[j, 0] = f_top
-        if not last:
+        if j < last:
+            hi[j, 0] = f_top
             nexts[0] = send(hi.at[j, 0], rec.at[j, 0], ss.at[j, 0], rs.at[j, 0], partners[j + 1])
-        for k, who in enumerate(peers):
-            arrivals.append(
-                send(hi.at[j, 0], out.at[j, z0, :, cols(core)], os_s.at[j, k], os_r.at[j, k], who)
-            )
-        out[j, z0, :, cols(core)] = f_top
+            out[j, z0, :, cols(core)] = f_top
+            for due in {3: (1, 2), 4: (3, 4), 5: (5,)}.get(j, ()):
+                publish(due)
         ways = nexts
+
+    a = ((LEVELS - 2) * 2 + z0) * 2 + bits[LEVELS - 2]
+    b = ((LEVELS - 1) * 2 + z0) * 2 + bits[LEVELS - 1]
+    o_seven = twice(op_g[a][:, :K], o_top, o_low)
+    h_eight = twice(op_h[b][:, :K], *split(o_seven))
+    f_seven = twice(op_s[a][:, :K], f_top, f_low) - twice(op_h[a][:, :K], o_top, o_low)
+    fin_s[1] = f_seven.astype(BF)
+    got_seven = send(fin_s.at[1], fin_r.at[3], fin_ss.at[3], fin_rs.at[3], partners[7])
+    f_eight = twice(op_s[b][:, :K], *split(f_seven)) - h_eight
+    fin_s[0] = f_eight.astype(BF)
+    got_eight = []
+    for k, who in ((1, partners[9]), (2, partners[8]), (0, partners[7])):
+        got_eight.append(send(fin_s.at[0], fin_r.at[k], fin_ss.at[k], fin_rs.at[k], who))
+    publish(last, f_top)
+    got_seven.wait_recv()
+    publish(LEVELS - 2, (f_seven + fin_r[3].astype(F32)).astype(BF))
+    for copy in got_eight:
+        copy.wait_recv()
+    for k in range(3):
+        f_eight = f_eight + fin_r[k].astype(F32)
+    publish(LEVELS - 1, f_eight.astype(BF))
     for copy in arrivals:
         copy.wait_recv()
     for copy in started:
@@ -377,7 +409,7 @@
             pltpu.VMEM((2, 2, 768), jnp.int32),
             pltpu.VMEM((768, 2304), BF),
             pltpu.VMEM((3, K, 768), BF),
-            pltpu.VMEM((3, K, 768), BF),
+            pltpu.VMEM((4, K, 768), BF),
             pltpu.VMEM((2, K, 768), BF),
             ops,
             ops,
@@ -393,6 +425,8 @@
             pltpu.VMEM((LEVELS, 4, K, 128), BF),
             pltpu.VMEM((4, K, 128), BF),
             pltpu.VMEM((LEVELS - 1, 2, K, 128), BF),
+            pltpu.VMEM((2, K, 128), BF),
+            pltpu.VMEM((4, K, 128), BF),
             dma((7,)),
             dma,
             dma,
@@ -406,20 +440,27 @@
             dma((LEVELS, 2)),
             dma((LEVELS, 3)),
             dma((LEVELS, 3)),
+            dma((4,)),
+            dma((4,)),
         ],
         compiler_params=pltpu.CompilerParams(
-            collective_id=0, has_side_effects=True, vmem_limit_bytes=56 << 20
+            collective_id=0, has_side_effects=True, vmem_limit_bytes=28 << 20
         ),
         name="window",
     )(
-        tile_cols,
-        omega,
-        adj_tests,
-        near_tiles,
-        leaf_perms,
-        jnp.swapaxes(leaf_interp, 2, 3),
-        node_perms,
-        node_maps,
+        *(
+            pltpu.with_memory_space_constraint(x, pltpu.HBM)
+            for x in (
+                tile_cols,
+                omega,
+                adj_tests,
+                near_tiles,
+                leaf_perms,
+                jnp.swapaxes(leaf_interp, 2, 3),
+                node_perms,
+                node_maps,
+            )
+        ),
     )[None]
 
 

time: 68.4 us -> 64.7 us (0.946)
  Pallas kernels: 66.1 us -> 63.6 us
  local copies, waits for them, and re-layouts: 2.14 us -> 0.91 us
    pallas_call x1, Pallas kernels: 66.1 us -> 63.6 us  [local(): pl.pallas_call(kernel, out_shape=jax.ShapeDtypeStruct((LEVELS, 2, K, 256)...]
    unnamed x1, local copies, waits for them, and re-layouts: 2.14 us -> 0.91 us
where the time goes in v4:
time: 64.7 us; the launch traced here: 64.6 us
  Pallas kernels  63.6 us (98%)
  local copies, waits for them, and re-layouts  0.91 us (1%)
    pallas_call x1, Pallas kernels, local(): pl.pallas_call(kernel, out_shape=jax.ShapeDtypeStruct((LEVELS, 2, K, 256)...  63.6 us

profile of v4, /device:TPU:1, one launch (start us, length us, event | category | flops | bytes accessed | tf_op | source)
XLA Modules:
  0.0 64.6 jit_solution(12359698071179441716)
XLA Ops:
  0.0 63.6 %window.1 = bf16[9,2,96,256]{3,2,1,0:T(8,128)(2,1)S(1)} custom-call(s32[6,12]{1,0:T(8,128)} %tile_cols.1, bf16[768,256]{1,0:T(8,128)(2,1)} %omega.1, bf16[4,49152]{1,0:T(4,128)(2,1)} %tests.1, bf16[6,12,128,128]{3,2,1,0:T(8,128)(2,1)} %near_in.1, s32[1,2,768]{2,1,0:T(2,128)} %leaf_perms.1, bf16[1,2,96,672]{3,2,1,0:T(8,128)(2,1)} %bitcast.3, ...), custom_call_target="tpu_custom_call" | custom-call | tf_op jit(solution)/shard_map/window/pallas_call | solution.py:392
  63.6 0.9 %copy.10 = bf16[1,9,2,96,256]{4,3,2,1,0:T(8,128)(2,1)} copy(bf16[1,9,2,96,256]{4,3,2,1,0:T(8,128)(2,1)S(1)} %bitcast.2) | data formatting | bytes 1769472

commit v5 on v4

--- a/solution.py
+++ b/solution.py
@@ -84,6 +84,18 @@
     bits = [core] + [lax.rem(z // b, 2) for b in (1, 2, 4)] + [lax.rem(x // b, 2) for b in (1, 2)]
     bits += [lax.rem(g // b, 2) for b in (1, 2, 4)]
 
+    barrier = pltpu.get_barrier_semaphore()
+
+    def greet(k, carry):
+        pl.semaphore_signal(
+            barrier, inc=1, device_id={"sub": lax.rem(s + k, 64)}, device_id_type=MESH
+        )
+        return carry
+
+    lax.fori_loop(1, 64, greet, 0)
+    for who in partners[6:]:
+        pl.semaphore_signal(barrier, inc=1, device_id=who, device_id_type=MESH)
+
     def fetch(src, dst, i):
         copy = pltpu.make_async_copy(src, dst, loc.at[i])
         copy.start()
@@ -96,18 +108,6 @@
     got_interp = fetch(interp_in.at[0], interp, 4)
     got_om = fetch(omega, om, 5)
     own_tests = fetch(tests.at[:, pl.ds(pl.multiple_of(s * 768, 768), 768)], adj_in.at[s], 6)
-
-    barrier = pltpu.get_barrier_semaphore()
-
-    def greet(k, carry):
-        pl.semaphore_signal(
-            barrier, inc=1, device_id={"sub": lax.rem(s + k, 64)}, device_id_type=MESH
-        )
-        return carry
-
-    lax.fori_loop(1, 64, greet, 0)
-    for who in partners[6:]:
-        pl.semaphore_signal(barrier, inc=1, device_id=who, device_id_type=MESH)
 
     got_nperm.wait()
     nrows[...] = jnp.zeros_like(nrows)
@@ -363,12 +363,12 @@
     h_eight = twice(op_h[b][:, :K], *split(o_seven))
     f_seven = twice(op_s[a][:, :K], f_top, f_low) - twice(op_h[a][:, :K], o_top, o_low)
     fin_s[1] = f_seven.astype(BF)
-    got_seven = send(fin_s.at[1], fin_r.at[3], fin_ss.at[3], fin_rs.at[3], partners[7])
     f_eight = twice(op_s[b][:, :K], *split(f_seven)) - h_eight
     fin_s[0] = f_eight.astype(BF)
     got_eight = []
     for k, who in ((1, partners[9]), (2, partners[8]), (0, partners[7])):
         got_eight.append(send(fin_s.at[0], fin_r.at[k], fin_ss.at[k], fin_rs.at[k], who))
+    got_seven = send(fin_s.at[1], fin_r.at[3], fin_ss.at[3], fin_rs.at[3], partners[7])
     publish(last, f_top)
     got_seven.wait_recv()
     publish(LEVELS - 2, (f_seven + fin_r[3].astype(F32)).astype(BF))

time: 64.7 us -> 64 us (0.989)
    pallas_call x1, Pallas kernels: 63.6 us -> 63 us  [local(): pl.pallas_call(kernel, out_shape=jax.ShapeDtypeStruct((LEVELS, 2, K, 256)...]
where the time goes in v5:
time: 64 us; the launch traced here: 63.9 us
  Pallas kernels  63 us (98%)
  local copies, waits for them, and re-layouts  0.91 us (1%)
    pallas_call x1, Pallas kernels, local(): pl.pallas_call(kernel, out_shape=jax.ShapeDtypeStruct((LEVELS, 2, K, 256)...  63 us

profile of v5, /device:TPU:1, one launch (start us, length us, event | category | flops | bytes accessed | tf_op | source)
XLA Modules:
  0.0 63.9 jit_solution(17531221300300587905)
XLA Ops:
  0.0 63.0 %window.1 = bf16[9,2,96,256]{3,2,1,0:T(8,128)(2,1)S(1)} custom-call(s32[6,12]{1,0:T(8,128)} %tile_cols.1, bf16[768,256]{1,0:T(8,128)(2,1)} %omega.1, bf16[4,49152]{1,0:T(4,128)(2,1)} %tests.1, bf16[6,12,128,128]{3,2,1,0:T(8,128)(2,1)} %near_in.1, s32[1,2,768]{2,1,0:T(2,128)} %leaf_perms.1, bf16[1,2,96,672]{3,2,1,0:T(8,128)(2,1)} %bitcast.3, ...), custom_call_target="tpu_custom_call" | custom-call | tf_op jit(solution)/shard_map/window/pallas_call | solution.py:392
  63.0 0.9 %copy.10 = bf16[1,9,2,96,256]{4,3,2,1,0:T(8,128)(2,1)} copy(bf16[1,9,2,96,256]{4,3,2,1,0:T(8,128)(2,1)S(1)} %bitcast.2) | data formatting | bytes 1769472

commit v6 on v5

--- a/solution.py
+++ b/solution.py
@@ -323,15 +323,16 @@
     started += ways
     f_top, o_top = hi[0, 2 * z0], hi[0, 2 * z0 + 1]
     f_low, o_low = lo[2 * z0], lo[2 * z0 + 1]
-    peers = ({"sub": mate}, {"sub": zmate}, {"sub": cross})
+    peers = ({"sub": cross}, {"sub": zmate}, {"sub": mate})
     def publish(j, top=None):
         if top is not None:
             hi[j, 0] = top
-            out[j, z0, :, cols(core)] = top
         for k, who in enumerate(peers):
             arrivals.append(
                 send(hi.at[j, 0], out.at[j, z0, :, cols(core)], os_s.at[j, k], os_r.at[j, k], who)
             )
+        if top is not None:
+            out[j, z0, :, cols(core)] = top
 
     last = LEVELS - 3
     for j in range(1, last + 1):

time: 64 us -> 63.7 us (level)
  no operation moved by 1% of the time
where the time goes in v6:
time: 63.7 us; the launch traced here: 63.6 us
  Pallas kernels  62.7 us (98%)
  local copies, waits for them, and re-layouts  0.91 us (1%)
    pallas_call x1, Pallas kernels, local(): pl.pallas_call(kernel, out_shape=jax.ShapeDtypeStruct((LEVELS, 2, K, 256)...  62.7 us

profile of v6, /device:TPU:1, one launch (start us, length us, event | category | flops | bytes accessed | tf_op | source)
XLA Modules:
  0.0 63.6 jit_solution(14382507087268051614)
XLA Ops:
  0.0 62.7 %window.1 = bf16[9,2,96,256]{3,2,1,0:T(8,128)(2,1)S(1)} custom-call(s32[6,12]{1,0:T(8,128)} %tile_cols.1, bf16[768,256]{1,0:T(8,128)(2,1)} %omega.1, bf16[4,49152]{1,0:T(4,128)(2,1)} %tests.1, bf16[6,12,128,128]{3,2,1,0:T(8,128)(2,1)} %near_in.1, s32[1,2,768]{2,1,0:T(2,128)} %leaf_perms.1, bf16[1,2,96,672]{3,2,1,0:T(8,128)(2,1)} %bitcast.3, ...), custom_call_target="tpu_custom_call" | custom-call | tf_op jit(solution)/shard_map/window/pallas_call | solution.py:393
  62.7 0.9 %copy.10 = bf16[1,9,2,96,256]{4,3,2,1,0:T(8,128)(2,1)} copy(bf16[1,9,2,96,256]{4,3,2,1,0:T(8,128)(2,1)S(1)} %bitcast.2) | data formatting | bytes 1769472
